TPU v7x, 128 devices: a whole 4x4x4 slice. The times are simulated.
128 devices in a mesh: samp: 8 (over z, y_lo), feat: 16 (over x, y_hi, core).
Axes of the slice: x: 4, y: 4 (y_hi: 2, y_lo: 2; y = y_hi * 2 + y_lo), z: 4, core: 2. Of those that a mesh axis runs over, the one named last changes fastest.
Arguments:
- design: bfloat16 [12288, 8192], P('samp', 'feat'), may hold values from -6 to 6
- labels: int32 [12288], P('samp'), may hold values 0 or 1
- coef_all: float32 [1048576], replicated, may hold values from -0.13 to 0.13
- active: int32 [8192], P('feat'), may hold values from 0 to 1048575, as said below
- penalty: float32 [8192], P('feat'), may hold values from 4 to 40
Outputs:
- gram: float32 [8192, 8192], P('samp', 'feat')
- gradient: float32 [8192], P('feat')
Inputs may be any that keep to these rules, and one draw needn't show every extreme that they name: `active`: the indices are distinct.
All inputs are finite; a program needn't handle non-finite values. No bound on the sum of `labels` on one device may be relied on, other than what follows from the above.
Results may differ from a plain program's by a relative error of at most 0.003.
Values may be sent and summed in bfloat16 or wider, within the bound.
No kernel may reach another device: no remote copies, remote signals or barrier semaphores. Data moves between devices by JAX's collectives and lax.ppermute only.
A program may use at most 128 MiB of HBM per device.

v0:
```python
import functools

import jax
import jax.numpy as jnp
from jax import lax
from jax.sharding import Mesh
from jax.sharding import PartitionSpec as P

SAMP = ("samp_0", "samp_1")
FEAT = ("feat_0", "feat_1", "feat_2")


def over_axes(x, axes):
    return functools.reduce(lax.psum, axes, x)


def copy_for_each(x, axis):
    copies = jnp.broadcast_to(x, (lax.axis_size(axis), *x.shape))
    return lax.all_to_all(copies, axis, split_axis=0, concat_axis=0, tiled=True)


def of_everyone(x, axis):
    return copy_for_each(x, axis).sum(axis=0)


def sum_by_axis(x, axes, dim):
    if not axes:
        return x
    nearer = lax.psum_scatter(x, axes[0], scatter_dimension=dim, tiled=True)
    return sum_by_axis(nearer, axes[1:], dim)


def per_device(design, labels, coef_all, active, penalty):
    rows = design.shape[0]
    total_rows = rows * lax.axis_size(SAMP)
    scale = 1.0 / jnp.sqrt(jnp.float32(total_rows))
    beta = coef_all[active]
    partial_margin = jnp.dot(design, beta.astype(jnp.bfloat16), preferred_element_type=jnp.float32)
    margin = over_axes(partial_margin, FEAT)
    prob = 1.0 / (1.0 + jnp.exp(-margin))
    weight = prob * (1.0 - prob)
    resid = prob - labels.astype(jnp.float32)
    weighted = (design.astype(jnp.float32) * weight[:, None]).astype(jnp.bfloat16)
    resid_b = resid.astype(jnp.bfloat16)
    grad_part = jnp.dot(resid_b, design, preferred_element_type=jnp.float32)
    gradient = of_everyone(grad_part, SAMP) * scale + penalty * beta
    terms = lax.dot_general(
        lax.all_gather(design, FEAT, axis=1, tiled=True),
        weighted,
        (((0,), (0,)), ((), ())),
        preferred_element_type=jnp.float32,
    )
    gram = sum_by_axis(terms, SAMP, 0) * scale
    return (gram, gradient)


def solution(mesh):
    split = Mesh(
        mesh.devices.reshape(4, 2, 4, 2, 2), ("samp_0", "samp_1", "feat_0", "feat_1", "feat_2")
    )
    placed = (P(SAMP, FEAT), P(SAMP), P(), P(FEAT), P(FEAT))
    return jax.shard_map(
        per_device, mesh=split, in_specs=placed, out_specs=(P(SAMP, FEAT), P(FEAT)), check_vma=False
    )
```

profile of v0, /device:TPU:1, one launch (start us, length us, event | category | flops | bytes accessed | tf_op | source)
XLA Modules:
  0.0 415.8 jit_solution(3469971202530513350)
XLA Ops:
  7.2 0.0 copy-start
  7.2 0.0 all-gather.2.cloned.1.call-start
  7.2 0.7 all-gather.2.cloned.1.call-update
  7.9 0.0 copy-start.1
  7.9 0.0 reduce-scatter.3.cloned.1.call-start
  8.0 0.7 compare_select_fusion
  8.7 6.5 %gather_fusion = f32[512]{0:T(512)S(1)} fusion(f32[1048576]{0:T(1024)} %param.7, s32[1024]{0:T(1024)S(1)} %pad_clamp_fusion), kind=kCustom, calls=%fused_computation | custom fusion | bytes 6144 | tf_op jit(solution)/shard_map/gather | solution.py:37
  15.2 0.0 copy-done
  15.2 0.5 convolution_reduce_fusion
  15.7 9.4 %psum.21 = f32[1536]{0:T(1024)S(1)} all-reduce(f32[1536]{0:T(1024)S(1)} %convolution_reduce_fusion), channel_id=1, replica_groups=mesh['samp_0'=4,'samp_1'=2,'feat_0'=4,'feat_1'=2,'feat_2'=2] {'feat_0'}, use_global_device_ids=true, to_apply=%region_0.0 | all-reduce | flops 1536 | bytes 12288 | tf_op jit(solution)/shard_map/psum | solution.py:14
  25.1 5.9 %psum.22 = f32[1536]{0:T(1024)S(1)} all-reduce(f32[1536]{0:T(1024)S(1)} %psum.21), channel_id=1, replica_groups=mesh['samp_0'=4,'samp_1'=2,'feat_0'=4,'feat_1'=2,'feat_2'=2] {'feat_1'}, use_global_device_ids=true, to_apply=%region_1.0 | all-reduce | flops 1536 | bytes 12288 | tf_op jit(solution)/shard_map/psum | solution.py:14
  31.0 5.8 %psum.23 = f32[1536]{0:T(1024)S(1)} all-reduce(f32[1536]{0:T(1024)S(1)} %psum.22), channel_id=1, replica_groups=mesh['samp_0'=4,'samp_1'=2,'feat_0'=4,'feat_1'=2,'feat_2'=2] {'feat_2'}, use_global_device_ids=true, to_apply=%region_2.0 | all-reduce | flops 1536 | bytes 12288 | tf_op jit(solution)/shard_map/psum | solution.py:14
  36.8 0.0 copy-done.1
  36.8 142.8 %all-gather.2.cloned.1.call-done = bf16[1536,8192]{1,0:T(8,128)(2,1)} async-done(((bf16[1536,512]{1,0:T(8,128)(2,1)}), bf16[1536,8192]{1,0:T(8,128)(2,1)}) %all-gather.2.cloned.1.call-update) | async-done | bytes 25165840 | tf_op jit(solution)/shard_map/all_gather | solution.py:48
  179.6 21.6 %convolution_bitcast_fusion = f32[8192,512]{0,1:T(8,128)} fusion(bf16[1536,8192]{1,0:T(8,128)(2,1)} %all-gather.2.cloned.1.call-done, bf16[1536,512]{1,0:T(8,128)(2,1)S(1)} %copy-done, f32[1536]{0:T(1024)S(1)} %get-tuple-element.11), kind=kOutput, calls=%fused_computation.1 | convolution fusion | flops 12887261184 | bytes 43522048 | tf_op jit(solution)/shard_map/dot_general | solution.py:47
  201.2 0.0 reduce-scatter.3.cloned.1.call-update
  201.3 0.0 reduce-scatter.5.cloned.1.call-start
  201.3 145.5 %reduce-scatter.3.cloned.1.call-done = f32[2048,512]{0,1:T(8,128)} async-done(((f32[8192,512]{0,1:T(8,128)}), f32[2048,512]{0,1:T(8,128)}) %reduce-scatter.3.cloned.1.call-update) | async-done | bytes 4194320 | tf_op jit(solution)/shard_map/reduce_scatter | solution.py:29
  346.8 0.0 copy-start.2
  346.8 0.0 reduce-scatter.5.cloned.1.call-update
  346.9 0.3 fusion.1
  347.2 8.2 %all_to_all.6 = f32[8,1,512]{2,1,0:T(1,128)S(1)} all-to-all(f32[8,1,512]{2,1,0:T(1,128)S(1)} %broadcast_in_dim.8), channel_id=1, replica_groups=mesh['samp_0'=4,'samp_1'=2,'feat_0'=4,'feat_1'=2,'feat_2'=2] {'samp_0','..., dimensions={0} | all-to-all | bytes 32768 | tf_op jit(solution)/shard_map/all_to_all | solution.py:19
  355.4 0.0 copy-done.2
  355.4 0.6 multiply_add_fusion
  356.0 49.6 %reduce-scatter.5.cloned.1.call-done = f32[1024,512]{0,1:T(8,128)} async-done(((f32[2048,512]{0,1:T(8,128)}), f32[1024,512]{0,1:T(8,128)}) %reduce-scatter.5.cloned.1.call-update) | async-done | bytes 2097168 | tf_op jit(solution)/shard_map/reduce_scatter | solution.py:29
  405.6 1.8 broadcast_multiply_fusion
  407.4 1.8 copy.11
  (7 shorter events, 0.1 us)
Async XLA Ops:
  7.2 8.0 %copy-start = (bf16[1536,512]{1,0:T(8,128)(2,1)S(1)}, bf16[1536,512]{1,0:T(8,128)(2,1)}, u32[]{:S(2)}) copy-start(bf16[1536,512]{1,0:T(8,128)(2,1)} %param.5) | copy-start | bytes 4718596
  7.2 172.4 %all-gather.2.cloned.1.call-start = ((), (), s32[]{:S(2)}) async-start(), calls=%async_computation.3 | async-start | bytes 26738688 | tf_op jit(solution)/shard_map/all_gather | solution.py:48
  7.9 28.9 %copy-start.1 = (s32[1536]{0:T(1024)S(1)}, s32[1536]{0:T(1024)}, u32[]{:S(2)}) copy-start(s32[1536]{0:T(1024)} %param.6) | copy-start | bytes 18436
  7.9 338.9 %reduce-scatter.3.cloned.1.call-start = ((), (), s32[]{:S(2)}) async-start(), calls=%async_computation.4 | async-start | bytes 20971520 | tf_op jit(solution)/shard_map/reduce_scatter | solution.py:29
  201.3 204.4 %reduce-scatter.5.cloned.1.call-start = ((), (), s32[]{:S(2)}) async-start(), calls=%async_computation.5 | async-start | bytes 6291456 | tf_op jit(solution)/shard_map/reduce_scatter | solution.py:29
  346.8 8.6 %copy-start.2 = (f32[512]{0:T(512)S(1)}, f32[512]{0:T(512)}, u32[]{:S(2)}) copy-start(f32[512]{0:T(512)} %param.9) | copy-start | bytes 6148
Sparse Core Ops, SparseCore 0:
  10.2 169.3 all-gather.1
  201.4 145.3 reduce-scatter.2
  349.2 56.3 reduce-scatter.4
where the time goes:
time: 416 us
  waiting for transfers between devices  339 us (81%)
  blocking collectives  29.3 us (7%)
  matrix products  22.5 us (5%)
  between operations  13.8 us (3%)
  local copies, waits for them, and re-layouts  8.36 us (2%)
    reduce_scatter x2, waiting for transfers between devices, sum_by_axis(): nearer = lax.psum_scatter(x, axes[0], scatter_dimension=dim, tiled=True)  195 us
    all_gather x1, waiting for transfers between devices, per_device(): lax.all_gather(design, FEAT, axis=1, tiled=True)  143 us
    dot_general x1, matrix products, per_device(): lax.dot_general(lax.all_gather(design, FEAT, axis=1, tiled=True), weighte...  21.6 us
    psum x3, blocking collectives, over_axes(): return functools.reduce(lax.psum, axes, x)  21 us
  transfers between devices with their start and end apart: 3, of which 3 were waited for; matrix products, arithmetic and copies ran while one was open for 2% of the time, Pallas kernels for 0%

commit v1 on v0

v1 whole, which is shorter than its diff:
```python
import itertools

import jax
import jax.numpy as jnp
from jax import lax
from jax.sharding import Mesh
from jax.sharding import PartitionSpec as P

AXES = ("z", "l", "x", "h", "c")
SAMP = ("z", "l")
FEAT = ("x", "h", "c")
SIZES = (4, 2, 4, 2, 2)
F32 = jnp.float32
BF16 = jnp.bfloat16


def send(value, route):
    pairs = []
    for source, at in enumerate(itertools.product(*map(range, SIZES))):
        target = route(*at)
        if target is not None:
            index = 0
            for size, place in zip(SIZES, target):
                index = index * size + place % size
            pairs.append((source, index))
    return lax.ppermute(value, AXES, pairs)


def core_swap(value):
    return send(value, lambda z, l, x, h, c: (z, l, x, h, 1 - c))


def near_route(z, l, x, h, c):
    return (z ^ 1 if c == 0 else 3 - z, l, x, h, c)


def over_route(z, l, x, h, c):
    return (3 - z if c == 0 else z ^ 1, l, x, h, c)


def sum_over_l(same, other, keeps):
    swapped = send(
        jnp.where(keeps, other, same).astype(BF16),
        lambda z, l, x, h, c: (z, h, x, 1 - h, c) if l == h else (z, h, x, h, c),
    )
    over = send(other.astype(BF16), lambda z, l, x, h, c: None if l == h else (z, h, x, 1 - h, c))
    return jnp.where(keeps, same, over.astype(F32)) + swapped.astype(F32)


def product(rows, weighted):
    return lax.dot_general(
        rows, weighted, (((0,), (0,)), ((), ())), preferred_element_type=F32
    ).astype(BF16)


def per_device(design, labels, coef_all, active, penalty):
    z, l, x, h, c = (lax.axis_index(name) for name in AXES)
    scale = 1.0 / jnp.sqrt(F32(design.shape[0] * 8))
    across = core_swap(design)
    beta = coef_all[active]
    part = jnp.dot(design, beta.astype(BF16), preferred_element_type=F32)
    part = part + core_swap(part)
    part = part + send(part, lambda z, l, x, h, c: (z, l, x, 1 - h, c))
    part = part + send(part, lambda z, l, x, h, c: (z, l, x ^ 1, h, c))
    margin = part + send(part, lambda z, l, x, h, c: (z, l, 3 - x, h, c))
    beside = send(design, lambda z, l, x, h, c: (z, l, x, 1 - h, c))
    ahead = send(design, lambda z, l, x, h, c: (z, l, x - 1, h, c))
    behind = send(design, lambda z, l, x, h, c: (z, l, x + 1, h, c))
    prob = 1.0 / (1.0 + jnp.exp(-margin))
    weight = prob * (1.0 - prob)
    resid_b = (prob - labels.astype(F32)).astype(BF16)
    grad = jnp.dot(resid_b, design, preferred_element_type=F32)
    grad = grad + send(grad, near_route)
    grad = grad + send(grad, over_route)
    grad = grad + send(grad, lambda z, l, x, h, c: (z, 1 - l, x, h, c))
    gradient = grad * scale + penalty * beta

    def weigh(block):
        return (block.astype(F32) * weight[:, None]).astype(BF16)

    both = lax.optimization_barrier(jnp.concatenate([weigh(design), weigh(beside)], axis=1))
    far = send(jnp.where(c == 0, behind, ahead), lambda z, l, x, h, c: (z, l, x + 1 - 2 * c, h, c))
    blocks = {
        0: (design, across),
        1: (ahead, core_swap(ahead)),
        3: (behind, core_swap(behind)),
        2: (far, core_swap(far)),
    }
    terms = [[product(blocks[j][r], both) for j in range(4)] for r in range(2)]

    def pick(r, place):
        j = (place - x) % 4
        first = jnp.where(j == 1, terms[r][1], terms[r][0])
        second = jnp.where(j == 3, terms[r][3], terms[r][2])
        return jnp.where(j >= 2, second, first)

    near = jnp.where(c == 0, z ^ 1, 3 - z)
    over = jnp.where(c == 0, 3 - z, z ^ 1)
    outs = []
    for r in range(2):
        far_side = send(pick(r, z ^ 2), near_route)
        near_side = send(pick(r, near), near_route)
        passed = pick(r, over).astype(F32) + far_side.astype(F32)
        over_side = send(passed.astype(BF16), over_route)
        total = pick(r, z).astype(F32) + near_side.astype(F32) + over_side.astype(F32)
        outs.append(sum_over_l(total[:, :512], total[:, 512:], l == h) * scale)
    first = jnp.where(c == 0, outs[0], outs[1])
    second = jnp.where(c == 0, outs[1], outs[0])
    return (jnp.concatenate([first, second], axis=0), gradient)


def solution(mesh):
    split = Mesh(mesh.devices.reshape(SIZES), AXES)
    placed = (P(SAMP, FEAT), P(SAMP), P(), P(FEAT), P(FEAT))

    return jax.shard_map(
        per_device, mesh=split, in_specs=placed, out_specs=(P(SAMP, FEAT), P(FEAT)), check_vma=False
    )
```

time: 416 us -> 190 us (0.46)
  the two profiles are of different devices: /device:TPU:1 before, /device:TPU:9 now
where the time goes in v1:
time: 190 us; the launch traced here: 189 us
  waiting for transfers between devices  97.6 us (51%)
  starting transfers between devices  39.1 us (21%)
  matrix products  24.5 us (13%)
  other arithmetic  20.2 us (11%)
  local copies, waits for them, and re-layouts  6.57 us (3%)
    ppermute x25, waiting for transfers between devices, send(): return lax.ppermute(value, AXES, pairs)  97.6 us
    ppermute x25, starting transfers between devices, send(): return lax.ppermute(value, AXES, pairs)  39.1 us
    dot_general x8, matrix products, product(): lax.dot_general(rows, weighted, (((0,), (0,)), ((), ())), preferred_eleme...  23.6 us
    convert_element_type x2, other arithmetic, per_device(): over_side = send(passed.astype(BF16), over_route)  7.57 us
    add x2, other arithmetic, per_device(): pick(r, z).astype(F32) + near_side.astype(F32) + over_side.astype(F32)  6.55 us
    gather x1, local copies, waits for them, and re-layouts, per_device(): beta = coef_all[active]  6.5 us
  transfers between devices with their start and end apart: 25, of which 13 were waited for; matrix products, arithmetic and copies ran while one was open for 26% of the time, Pallas kernels for 0%

profile of v1, /device:TPU:9, one launch (start us, length us, event | category | flops | bytes accessed | tf_op | source)
XLA Modules:
  0.0 188.9 jit_solution(11977694887379851759)
XLA Ops:
  0.6 2.5 %collective-permute-start.6 = (bf16[1536,512]{1,0:T(8,128)(2,1)}, bf16[1536,512]{1,0:T(8,128)(2,1)}, u32[]{:S(2)}, u32[]{:S(2)}) collective-permute-start(bf16[1536,512]{1,0:T(8,128)(2,1)} %param.5), channel_id=1, source_target_pairs={{0,12},{1,13},{2,14},{3,15},{4,0},{5,1},{6,2},{7,3},{8,4},{9,5},{1... | collective-permute-start | bytes 4718600 | tf_op jit(solution)/shard_map/ppermute | solution.py:26
  3.2 2.0 %collective-permute-start.4 = (bf16[1536,512]{1,0:T(8,128)(2,1)}, bf16[1536,512]{1,0:T(8,128)(2,1)S(1)}, u32[]{:S(2)}, u32[]{:S(2)}) collective-permute-start(bf16[1536,512]{1,0:T(8,128)(2,1)} %param.5), channel_id=1, source_target_pairs={{0,2},{1,3},{2,0},{3,1},{4,6},{5,7},{6,4},{7,5},{8,10},{9,11},{10,... | collective-permute-start | bytes 4718600 | tf_op jit(solution)/shard_map/ppermute | solution.py:26
  5.2 0.7 compare_select_fusion
  5.9 6.5 %gather_fusion = f32[512]{0:T(512)S(1)} fusion(f32[1048576]{0:T(1024)} %param.7, s32[1024]{0:T(1024)S(1)} %pad_clamp_fusion), kind=kCustom, calls=%fused_computation | custom fusion | bytes 6144 | tf_op jit(solution)/shard_map/gather | solution.py:60
  12.5 0.5 convolution_reduce_fusion
  13.0 1.3 collective-permute-start
  14.3 0.8 collective-permute-done
  15.1 1.0 collective-permute-start.1
  16.1 24.1 %collective-permute-done.1 = f32[1536]{0:T(1024)S(1)} collective-permute-done((f32[1536]{0:T(1024)S(1)}, f32[1536]{0:T(1024)S(1)}, u32[]{:S(2)}, u32[]{:S(2)}) %collective-permute-start.1) | collective-permute-done | bytes 6176 | tf_op jit(solution)/shard_map/ppermute | solution.py:26
  40.2 2.5 %collective-permute-done.2 = f32[1536]{0:T(1024)S(1)} collective-permute-done((f32[1536]{0:T(1024)S(1)}, f32[1536]{0:T(1024)S(1)}, u32[]{:S(2)}, u32[]{:S(2)}) %collective-permute-start.2) | collective-permute-done | bytes 6176 | tf_op jit(solution)/shard_map/ppermute | solution.py:26
  42.7 2.3 %collective-permute-start.3 = (f32[1536]{0:T(1024)S(1)}, f32[1536]{0:T(1024)S(1)}, u32[]{:S(2)}, u32[]{:S(2)}) collective-permute-start(f32[1536]{0:T(1024)S(1)} %add.79), channel_id=1, source_target_pairs={{0,12},{1,13},{2,14},{3,15},{4,8},{5,9},{6,10},{7,11},{8,4},{9,5},... | collective-permute-start | bytes 18440 | tf_op jit(solution)/shard_map/ppermute | solution.py:26
  45.0 3.5 %collective-permute-start.16 = (bf16[1536,512]{1,0:T(8,128)(2,1)S(1)}, bf16[1536,512]{1,0:T(8,128)(2,1)}, u32[]{:S(2)}, u32[]{:S(2)}) collective-permute-start(bf16[1536,512]{1,0:T(8,128)(2,1)S(1)} %copy-done), channel_id=1, source_target_pairs={{0,1},{1,0},{2,3},{3,2},{4,5},{5,4},{6,7},{7,6},{8,9},{9,8},{10,11... | collective-permute-start | bytes 4718600 | tf_op jit(solution)/shard_map/ppermute | solution.py:26
  48.6 1.6 broadcast_select_fusion
  50.4 0.6 multiply_convert_fusion.1
  51.5 1.8 collective-permute-start.15
  53.4 1.9 convolution_convert_fusion.4
  55.3 3.6 %fusion = bf16[512,1024]{1,0:T(8,128)(2,1)S(1)} fusion(bf16[1536,1024]{1,0:T(8,128)(2,1)S(1)} %pad_maximum_fusion, bf16[1536,512]{1,0:T(8,128)(2,1)} %collective-permute-done.5), kind=kOutput, calls=%fused_computation.18 | convolution fusion | flops 1611137024 | bytes 5767168 | tf_op jit(solution)/shard_map/dot_general | solution.py:51
  58.9 3.6 %convolution_convert_fusion = bf16[1024,512]{0,1:T(8,128)(2,1)S(1)} fusion(bf16[1536,1024]{1,0:T(8,128)(2,1)S(1)} %pad_maximum_fusion, bf16[1536,512]{1,0:T(8,128)(2,1)} %collective-permute-done.16), kind=kOutput, calls=%fused_computation.10 | convolution fusion | flops 1611137024 | bytes 5767168 | tf_op jit(solution)/shard_map/dot_general | solution.py:51
  62.6 7.2 %collective-permute-done.7 = bf16[1536,512]{1,0:T(8,128)(2,1)S(1)} collective-permute-done((bf16[1536,512]{1,0:T(8,128)(2,1)S(1)}, bf16[1536,512]{1,0:T(8,128)(2,1)S(1)}, u32[]{:S(2)}, u32[]{:S(2)}) %collective-permute-start.7) | collective-permute-done | bytes 1572896 | tf_op jit(solution)/shard_map/ppermute | solution.py:26
  69.8 4.0 %collective-permute-start.14 = (bf16[1536,512]{1,0:T(8,128)(2,1)S(1)}, bf16[1536,512]{1,0:T(8,128)(2,1)S(1)}, u32[]{:S(2)}, u32[]{:S(2)}) collective-permute-start(bf16[1536,512]{1,0:T(8,128)(2,1)S(1)} %collective-permute-done.7), channel_id=1, source_target_pairs={{0,1},{1,0},{2,3},{3,2},{4,5},{5,4},{6,7},{7,6},{8,9},{9,8},{10,11... | collective-permute-start | bytes 4718600 | tf_op jit(solution)/shard_map/ppermute | solution.py:26
  73.7 1.8 convolution_convert_fusion.6
  75.6 5.4 %bitcast_select_fusion.6 = (bf16[512,1024]{1,0:T(8,128)(2,1)}, bf16[512,1024]{1,0:T(8,128)(2,1)}, bf16[1024,512]{0,1:T(8,128)(2,1)}) fusion(bf16[1024,512]{0,1:T(8,128)(2,1)S(1)} %convolution_convert_fusion.4, bf16[512,1024]{1,0:T(8,128)(2,1)S(1)} %fusion, bf16[512,1024]{1,0:T(8,128)(2,1)S(1)} %convolution_convert_fusion.6, pred[]{:T(512)S(6)} %eq.57, ...), kind=kOutput, calls=%fused_computation.27 | convolution fusion | flops 1614282752 | bytes 11010054 | tf_op jit(solution)/shard_map/dot_general | solution.py:51
  81.0 3.8 %collective-permute-start.9 = (bf16[512,1024]{1,0:T(8,128)(2,1)}, bf16[512,1024]{1,0:T(8,128)(2,1)}, u32[]{:S(2)}, u32[]{:S(2)}) collective-permute-start(bf16[512,1024]{1,0:T(8,128)(2,1)} %get-tuple-element.7), channel_id=1, source_target_pairs={{0,32},{1,97},{2,34},{3,99},{4,36},{5,101},{6,38},{7,103},{8,40},{... | collective-permute-start | bytes 3145736 | tf_op jit(solution)/shard_map/ppermute | solution.py:26
  84.7 1.9 fusion.1
  86.6 1.8 convolution_convert_fusion.2
  88.5 3.6 %bitcast_select_fusion.2 = (bf16[512,1024]{1,0:T(8,128)(2,1)}, bf16[512,1024]{1,0:T(8,128)(2,1)}, bf16[1024,512]{0,1:T(8,128)(2,1)}) fusion(bf16[1024,512]{0,1:T(8,128)(2,1)S(1)} %convolution_convert_fusion, bf16[512,1024]{1,0:T(8,128)(2,1)S(1)} %fusion.1, bf16[512,1024]{1,0:T(8,128)(2,1)S(1)} %convolution_convert_fusion.2, pred[]{:T(512)S(6)} %eq.57, ...), kind=kOutput, calls=%fused_computation.23 | convolution fusion | flops 1614282752 | bytes 11010054 | tf_op jit(solution)/shard_map/dot_general | solution.py:51
  92.1 2.7 %collective-permute-start.8 = (bf16[512,1024]{1,0:T(8,128)(2,1)}, bf16[512,1024]{1,0:T(8,128)(2,1)}, u32[]{:S(2)}, u32[]{:S(2)}) collective-permute-start(bf16[512,1024]{1,0:T(8,128)(2,1)} %get-tuple-element.6), channel_id=1, source_target_pairs={{0,32},{1,97},{2,34},{3,99},{4,36},{5,101},{6,38},{7,103},{8,40},{... | collective-permute-start | bytes 3145736 | tf_op jit(solution)/shard_map/ppermute | solution.py:26
  94.8 2.4 %collective-permute-done.9 = bf16[512,1024]{1,0:T(8,128)(2,1)} collective-permute-done((bf16[512,1024]{1,0:T(8,128)(2,1)}, bf16[512,1024]{1,0:T(8,128)(2,1)}, u32[]{:S(2)}, u32[]{:S(2)}) %collective-permute-start.9) | collective-permute-done | bytes 1048608 | tf_op jit(solution)/shard_map/ppermute | solution.py:26
  97.2 4.2 %add_convert_fusion.1 = bf16[512,1024]{1,0:T(8,128)(2,1)} fusion(bf16[512,1024]{1,0:T(8,128)(2,1)} %collective-permute-done.9, bf16[1024,512]{0,1:T(8,128)(2,1)} %get-tuple-element.16, bf16[1024,512]{0,1:T(8,128)(2,1)} %copy-done.1, bf16[512,1024]{1,0:T(8,128)(2,1)} %copy-done.2, bf16[512,1024]{1,0:T(8,128)(2,1)} %copy-done.9, pred[]{:T(512)S(6)} %eq.59, ...), kind=kLoop, calls=%fused_computation.8 | loop fusion | flops 3670016 | bytes 6291459 | tf_op jit(solution)/shard_map/convert_element_type | solution.py:104
  101.4 2.7 %collective-permute-start.17 = (bf16[512,1024]{1,0:T(8,128)(2,1)}, bf16[512,1024]{1,0:T(8,128)(2,1)}, u32[]{:S(2)}, u32[]{:S(2)}) collective-permute-start(bf16[512,1024]{1,0:T(8,128)(2,1)} %get-tuple-element.4), channel_id=1, source_target_pairs={{0,32},{1,97},{2,34},{3,99},{4,36},{5,101},{6,38},{7,103},{8,40},{... | collective-permute-start | bytes 3145736 | tf_op jit(solution)/shard_map/ppermute | solution.py:26
  104.1 7.6 %collective-permute-done.18 = bf16[512,1024]{1,0:T(8,128)(2,1)} collective-permute-done((bf16[512,1024]{1,0:T(8,128)(2,1)}, bf16[512,1024]{1,0:T(8,128)(2,1)}, u32[]{:S(2)}, u32[]{:S(2)}) %collective-permute-start.18) | collective-permute-done | bytes 1048608 | tf_op jit(solution)/shard_map/ppermute | solution.py:26
  111.7 3.4 %add_convert_fusion = bf16[512,1024]{1,0:T(8,128)(2,1)} fusion(bf16[512,1024]{1,0:T(8,128)(2,1)} %collective-permute-done.18, bf16[1024,512]{0,1:T(8,128)(2,1)S(1)} %copy-done.10, bf16[1024,512]{0,1:T(8,128)(2,1)S(1)} %convolution_convert_fusion, bf16[512,1024]{1,0:T(8,128)(2,1)S(1)} %copy-done.4, bf16[512,1024]{1,0:T(8,128)(2,1)S(1)} %copy-done.7, ...), kind=kLoop, calls=%fused_computation.6 | loop fusion | flops 3670016 | bytes 6291459 | tf_op jit(solution)/shard_map/convert_element_type | solution.py:104
  115.1 19.1 %collective-permute-done.8 = bf16[512,1024]{1,0:T(8,128)(2,1)} collective-permute-done((bf16[512,1024]{1,0:T(8,128)(2,1)}, bf16[512,1024]{1,0:T(8,128)(2,1)}, u32[]{:S(2)}, u32[]{:S(2)}) %collective-permute-start.8) | collective-permute-done | bytes 1048608 | tf_op jit(solution)/shard_map/ppermute | solution.py:26
  134.2 3.6 %convert_add_fusion.1 = f32[512,1024]{1,0:T(8,128)S(1)} fusion(bf16[512,1024]{1,0:T(8,128)(2,1)} %collective-permute-done.10, bf16[512,1024]{1,0:T(8,128)(2,1)} %collective-permute-done.8, bf16[1024,512]{0,1:T(8,128)(2,1)} %get-tuple-element.16, bf16[1024,512]{0,1:T(8,128)(2,1)} %copy-done.1, bf16[512,1024]{1,0:T(8,128)(2,1)} %copy-done.2, ...), kind=kLoop, calls=%fused_computation.7 | loop fusion | flops 4194304 | bytes 8388611 | tf_op jit(solution)/shard_map/add | solution.py:105
  138.0 3.3 %collective-permute-start.11 = (bf16[512,512]{1,0:T(8,128)(2,1)S(1)}, bf16[512,512]{1,0:T(8,128)(2,1)S(1)}, u32[]{:S(2)}, u32[]{:S(2)}) collective-permute-start(bf16[512,512]{1,0:T(8,128)(2,1)S(1)} %get-tuple-element.10), channel_id=1, source_target_pairs={{2,16},{3,17},{6,20},{7,21},{10,24},{11,25},{14,28},{15,29},{16,2}... | collective-permute-start | bytes 1572872 | tf_op jit(solution)/shard_map/ppermute | solution.py:26
  141.4 12.0 %collective-permute-done.17 = bf16[512,1024]{1,0:T(8,128)(2,1)} collective-permute-done((bf16[512,1024]{1,0:T(8,128)(2,1)}, bf16[512,1024]{1,0:T(8,128)(2,1)}, u32[]{:S(2)}, u32[]{:S(2)}) %collective-permute-start.17) | collective-permute-done | bytes 1048608 | tf_op jit(solution)/shard_map/ppermute | solution.py:26
  153.4 2.9 %convert_add_fusion = f32[512,1024]{1,0:T(8,128)S(1)} fusion(bf16[512,1024]{1,0:T(8,128)(2,1)} %collective-permute-done.19, bf16[512,1024]{1,0:T(8,128)(2,1)} %collective-permute-done.17, bf16[1024,512]{0,1:T(8,128)(2,1)S(1)} %copy-done.11, bf16[1024,512]{0,1:T(8,128)(2,1)S(1)} %convolution_convert_fusion, bf16[512,1024]{1,0:T(8,128)(2,1)S(1)} %copy-done.5, ...), kind=kLoop, calls=%fused_computation.5 | loop fusion | flops 4194304 | bytes 8388611 | tf_op jit(solution)/shard_map/add | solution.py:105
  156.5 3.2 %collective-permute-start.20 = (bf16[512,512]{1,0:T(8,128)(2,1)S(1)}, bf16[512,512]{1,0:T(8,128)(2,1)S(1)}, u32[]{:S(2)}, u32[]{:S(2)}) collective-permute-start(bf16[512,512]{1,0:T(8,128)(2,1)S(1)} %get-tuple-element.8), channel_id=1, source_target_pairs={{2,16},{3,17},{6,20},{7,21},{10,24},{11,25},{14,28},{15,29},{16,2}... | collective-permute-start | bytes 1572872 | tf_op jit(solution)/shard_map/ppermute | solution.py:26
  160.1 2.7 %collective-permute-start.22 = (f32[512]{0:T(512)S(1)}, f32[512]{0:T(512)S(1)}, u32[]{:S(2)}, u32[]{:S(2)}) collective-permute-start(f32[512]{0:T(512)S(1)} %bitcast.49), channel_id=1, source_target_pairs={{0,32},{1,97},{2,34},{3,99},{4,36},{5,101},{6,38},{7,103},{8,40},{... | collective-permute-start | bytes 6152 | tf_op jit(solution)/shard_map/ppermute | solution.py:26
  162.8 1.1 collective-permute-done.22
  163.9 2.7 %collective-permute-done.23 = f32[512]{0:T(512)S(1)} collective-permute-done((f32[512]{0:T(512)S(1)}, f32[512]{0:T(512)S(1)}, u32[]{:S(2)}, u32[]{:S(2)}) %collective-permute-start.23) | collective-permute-done | bytes 2080 | tf_op jit(solution)/shard_map/ppermute | solution.py:26
  166.6 1.8 collective-permute-start.24
  168.4 5.4 %collective-permute-done.24 = f32[512]{0:T(512)S(1)} collective-permute-done((f32[512]{0:T(512)S(1)}, f32[512]{0:T(512)S(1)}, u32[]{:S(2)}, u32[]{:S(2)}) %collective-permute-start.24) | collective-permute-done | bytes 2080 | tf_op jit(solution)/shard_map/ppermute | solution.py:26
  173.9 0.6 multiply_add_fusion
  174.4 2.0 %collective-permute-done.11 = bf16[512,512]{1,0:T(8,128)(2,1)S(1)} collective-permute-done((bf16[512,512]{1,0:T(8,128)(2,1)S(1)}, bf16[512,512]{1,0:T(8,128)(2,1)S(1)}, u32[]{:S(2)}, u32[]{:S(2)}) %collective-permute-start.11) | collective-permute-done | bytes 524320 | tf_op jit(solution)/shard_map/ppermute | solution.py:26
  176.4 10.5 %collective-permute-done.20 = bf16[512,512]{1,0:T(8,128)(2,1)S(1)} collective-permute-done((bf16[512,512]{1,0:T(8,128)(2,1)S(1)}, bf16[512,512]{1,0:T(8,128)(2,1)S(1)}, u32[]{:S(2)}, u32[]{:S(2)}) %collective-permute-start.20) | collective-permute-done | bytes 524320 | tf_op jit(solution)/shard_map/ppermute | solution.py:26
  187.0 0.5 broadcast_select_fusion.2
  187.4 1.5 pad_maximum_fusion.1
  (64 shorter events, 1.7 us)
Async XLA Ops:
  0.6 11.8 %copy-start = (bf16[1536,512]{1,0:T(8,128)(2,1)S(1)}, bf16[1536,512]{1,0:T(8,128)(2,1)}, u32[]{:S(2)}) copy-start(bf16[1536,512]{1,0:T(8,128)(2,1)} %param.5) | copy-start | bytes 4718596
  0.6 47.9 %copy-start.12 = (s32[1536]{0:T(1024)S(1)}, s32[1536]{0:T(1024)}, u32[]{:S(2)}) copy-start(s32[1536]{0:T(1024)} %param.6) | copy-start | bytes 18436
  0.6 47.9 %collective-permute-start.6 = (bf16[1536,512]{1,0:T(8,128)(2,1)}, bf16[1536,512]{1,0:T(8,128)(2,1)}, u32[]{:S(2)}, u32[]{:S(2)}) collective-permute-start(bf16[1536,512]{1,0:T(8,128)(2,1)} %param.5), channel_id=1, source_target_pairs={{0,12},{1,13},{2,14},{3,15},{4,0},{5,1},{6,2},{7,3},{8,4},{9,5},{1... | collective-permute-start | bytes 4718600 | tf_op jit(solution)/shard_map/ppermute | solution.py:26
  3.2 45.4 %collective-permute-start.5 = (bf16[1536,512]{1,0:T(8,128)(2,1)}, bf16[1536,512]{1,0:T(8,128)(2,1)}, u32[]{:S(2)}, u32[]{:S(2)}) collective-permute-start(bf16[1536,512]{1,0:T(8,128)(2,1)} %param.5), channel_id=1, source_target_pairs={{0,4},{1,5},{2,6},{3,7},{4,8},{5,9},{6,10},{7,11},{8,12},{9,13},{1... | collective-permute-start | bytes 4718600 | tf_op jit(solution)/shard_map/ppermute | solution.py:26
  3.2 47.2 %collective-permute-start.4 = (bf16[1536,512]{1,0:T(8,128)(2,1)}, bf16[1536,512]{1,0:T(8,128)(2,1)S(1)}, u32[]{:S(2)}, u32[]{:S(2)}) collective-permute-start(bf16[1536,512]{1,0:T(8,128)(2,1)} %param.5), channel_id=1, source_target_pairs={{0,2},{1,3},{2,0},{3,1},{4,6},{5,7},{6,4},{7,5},{8,10},{9,11},{10,... | collective-permute-start | bytes 4718600 | tf_op jit(solution)/shard_map/ppermute | solution.py:26
  13.0 2.1 %collective-permute-start = (f32[1536]{0:T(1024)S(1)}, f32[1536]{0:T(1024)S(1)}, u32[]{:S(2)}, u32[]{:S(2)}) collective-permute-start(f32[1536]{0:T(1024)S(1)} %convolution_reduce_fusion), channel_id=1, source_target_pairs={{0,1},{1,0},{2,3},{3,2},{4,5},{5,4},{6,7},{7,6},{8,9},{9,8},{10,11... | collective-permute-start | bytes 18440 | tf_op jit(solution)/shard_map/ppermute | solution.py:26
  15.1 25.1 %collective-permute-start.1 = (f32[1536]{0:T(1024)S(1)}, f32[1536]{0:T(1024)S(1)}, u32[]{:S(2)}, u32[]{:S(2)}) collective-permute-start(f32[1536]{0:T(1024)S(1)} %add.77), channel_id=1, source_target_pairs={{0,2},{1,3},{2,0},{3,1},{4,6},{5,7},{6,4},{7,5},{8,10},{9,11},{10,... | collective-permute-start | bytes 18440 | tf_op jit(solution)/shard_map/ppermute | solution.py:26
  40.2 2.5 %collective-permute-start.2 = (f32[1536]{0:T(1024)S(1)}, f32[1536]{0:T(1024)S(1)}, u32[]{:S(2)}, u32[]{:S(2)}) collective-permute-start(f32[1536]{0:T(1024)S(1)} %add.78), channel_id=1, source_target_pairs={{0,4},{1,5},{2,6},{3,7},{4,0},{5,1},{6,2},{7,3},{8,12},{9,13},{10,... | collective-permute-start | bytes 18440 | tf_op jit(solution)/shard_map/ppermute | solution.py:26
  42.7 5.8 %collective-permute-start.3 = (f32[1536]{0:T(1024)S(1)}, f32[1536]{0:T(1024)S(1)}, u32[]{:S(2)}, u32[]{:S(2)}) collective-permute-start(f32[1536]{0:T(1024)S(1)} %add.79), channel_id=1, source_target_pairs={{0,12},{1,13},{2,14},{3,15},{4,8},{5,9},{6,10},{7,11},{8,4},{9,5},... | collective-permute-start | bytes 18440 | tf_op jit(solution)/shard_map/ppermute | solution.py:26
  45.0 13.9 %collective-permute-start.16 = (bf16[1536,512]{1,0:T(8,128)(2,1)S(1)}, bf16[1536,512]{1,0:T(8,128)(2,1)}, u32[]{:S(2)}, u32[]{:S(2)}) collective-permute-start(bf16[1536,512]{1,0:T(8,128)(2,1)S(1)} %copy-done), channel_id=1, source_target_pairs={{0,1},{1,0},{2,3},{3,2},{4,5},{5,4},{6,7},{7,6},{8,9},{9,8},{10,11... | collective-permute-start | bytes 4718600 | tf_op jit(solution)/shard_map/ppermute | solution.py:26
  50.1 19.6 %collective-permute-start.7 = (bf16[1536,512]{1,0:T(8,128)(2,1)S(1)}, bf16[1536,512]{1,0:T(8,128)(2,1)S(1)}, u32[]{:S(2)}, u32[]{:S(2)}) collective-permute-start(bf16[1536,512]{1,0:T(8,128)(2,1)S(1)} %broadcast_select_fusion), channel_id=1, source_target_pairs={{0,4},{1,13},{2,6},{3,15},{4,8},{5,1},{6,10},{7,3},{8,12},{9,5},{1... | collective-permute-start | bytes 4718600 | tf_op jit(solution)/shard_map/ppermute | solution.py:26
  51.5 37.0 %collective-permute-start.15 = (bf16[1536,512]{1,0:T(8,128)(2,1)}, bf16[1536,512]{1,0:T(8,128)(2,1)S(1)}, u32[]{:S(2)}, u32[]{:S(2)}) collective-permute-start(bf16[1536,512]{1,0:T(8,128)(2,1)} %collective-permute-done.6), channel_id=1, source_target_pairs={{0,1},{1,0},{2,3},{3,2},{4,5},{5,4},{6,7},{7,6},{8,9},{9,8},{10,11... | collective-permute-start | bytes 4718600 | tf_op jit(solution)/shard_map/ppermute | solution.py:26
  53.3 31.4 %collective-permute-start.13 = (bf16[1536,512]{1,0:T(8,128)(2,1)}, bf16[1536,512]{1,0:T(8,128)(2,1)S(1)}, u32[]{:S(2)}, u32[]{:S(2)}) collective-permute-start(bf16[1536,512]{1,0:T(8,128)(2,1)} %collective-permute-done.5), channel_id=1, source_target_pairs={{0,1},{1,0},{2,3},{3,2},{4,5},{5,4},{6,7},{7,6},{8,9},{9,8},{10,11... | collective-permute-start | bytes 4718600 | tf_op jit(solution)/shard_map/ppermute | solution.py:26
  55.3 20.3 %copy-start.1 = (bf16[1024,512]{0,1:T(8,128)(2,1)}, bf16[1024,512]{0,1:T(8,128)(2,1)S(1)}, u32[]{:S(2)}) copy-start(bf16[1024,512]{0,1:T(8,128)(2,1)S(1)} %convolution_convert_fusion.4) | copy-start | bytes 3145732
  58.9 16.6 %copy-start.2 = (bf16[512,1024]{1,0:T(8,128)(2,1)}, bf16[512,1024]{1,0:T(8,128)(2,1)S(1)}, u32[]{:S(2)}) copy-start(bf16[512,1024]{1,0:T(8,128)(2,1)S(1)} %fusion) | copy-start | bytes 3145732
  69.8 16.8 %collective-permute-start.14 = (bf16[1536,512]{1,0:T(8,128)(2,1)S(1)}, bf16[1536,512]{1,0:T(8,128)(2,1)S(1)}, u32[]{:S(2)}, u32[]{:S(2)}) collective-permute-start(bf16[1536,512]{1,0:T(8,128)(2,1)S(1)} %collective-permute-done.7), channel_id=1, source_target_pairs={{0,1},{1,0},{2,3},{3,2},{4,5},{5,4},{6,7},{7,6},{8,9},{9,8},{10,11... | collective-permute-start | bytes 4718600 | tf_op jit(solution)/shard_map/ppermute | solution.py:26
  75.6 5.4 %copy-start.9 = (bf16[512,1024]{1,0:T(8,128)(2,1)}, bf16[512,1024]{1,0:T(8,128)(2,1)S(1)}, u32[]{:S(2)}) copy-start(bf16[512,1024]{1,0:T(8,128)(2,1)S(1)} %convolution_convert_fusion.6) | copy-start | bytes 3145732
  81.0 16.3 %collective-permute-start.9 = (bf16[512,1024]{1,0:T(8,128)(2,1)}, bf16[512,1024]{1,0:T(8,128)(2,1)}, u32[]{:S(2)}, u32[]{:S(2)}) collective-permute-start(bf16[512,1024]{1,0:T(8,128)(2,1)} %get-tuple-element.7), channel_id=1, source_target_pairs={{0,32},{1,97},{2,34},{3,99},{4,36},{5,101},{6,38},{7,103},{8,40},{... | collective-permute-start | bytes 3145736 | tf_op jit(solution)/shard_map/ppermute | solution.py:26
  86.6 1.9 copy-start.3
  88.4 3.7 %copy-start.6 = (bf16[512,1024]{1,0:T(8,128)(2,1)}, bf16[512,1024]{1,0:T(8,128)(2,1)S(1)}, u32[]{:S(2)}) copy-start(bf16[512,1024]{1,0:T(8,128)(2,1)S(1)} %convolution_convert_fusion.2) | copy-start | bytes 3145732
  92.1 19.6 %collective-permute-start.18 = (bf16[512,1024]{1,0:T(8,128)(2,1)}, bf16[512,1024]{1,0:T(8,128)(2,1)}, u32[]{:S(2)}, u32[]{:S(2)}) collective-permute-start(bf16[512,1024]{1,0:T(8,128)(2,1)} %get-tuple-element.5), channel_id=1, source_target_pairs={{0,32},{1,97},{2,34},{3,99},{4,36},{5,101},{6,38},{7,103},{8,40},{... | collective-permute-start | bytes 3145736 | tf_op jit(solution)/shard_map/ppermute | solution.py:26
  92.1 42.1 %collective-permute-start.8 = (bf16[512,1024]{1,0:T(8,128)(2,1)}, bf16[512,1024]{1,0:T(8,128)(2,1)}, u32[]{:S(2)}, u32[]{:S(2)}) collective-permute-start(bf16[512,1024]{1,0:T(8,128)(2,1)} %get-tuple-element.6), channel_id=1, source_target_pairs={{0,32},{1,97},{2,34},{3,99},{4,36},{5,101},{6,38},{7,103},{8,40},{... | collective-permute-start | bytes 3145736 | tf_op jit(solution)/shard_map/ppermute | solution.py:26
  97.2 14.5 %copy-start.4 = (bf16[512,1024]{1,0:T(8,128)(2,1)S(1)}, bf16[512,1024]{1,0:T(8,128)(2,1)}, u32[]{:S(2)}) copy-start(bf16[512,1024]{1,0:T(8,128)(2,1)} %copy-done.3) | copy-start | bytes 3145732
  97.2 14.5 %copy-start.7 = (bf16[512,1024]{1,0:T(8,128)(2,1)S(1)}, bf16[512,1024]{1,0:T(8,128)(2,1)}, u32[]{:S(2)}) copy-start(bf16[512,1024]{1,0:T(8,128)(2,1)} %copy-done.6) | copy-start | bytes 3145732
  97.2 14.5 %copy-start.10 = (bf16[1024,512]{0,1:T(8,128)(2,1)S(1)}, bf16[1024,512]{0,1:T(8,128)(2,1)}, u32[]{:S(2)}) copy-start(bf16[1024,512]{0,1:T(8,128)(2,1)} %get-tuple-element.17) | copy-start | bytes 3145732
  101.4 32.8 %collective-permute-start.10 = (bf16[512,1024]{1,0:T(8,128)(2,1)}, bf16[512,1024]{1,0:T(8,128)(2,1)}, u32[]{:S(2)}, u32[]{:S(2)}) collective-permute-start(bf16[512,1024]{1,0:T(8,128)(2,1)} %add_convert_fusion.1), channel_id=1, source_target_pairs={{0,96},{1,33},{2,98},{3,35},{4,100},{5,37},{6,102},{7,39},{8,104},... | collective-permute-start | bytes 3145736 | tf_op jit(solution)/shard_map/ppermute | solution.py:26
  101.4 52.0 %collective-permute-start.17 = (bf16[512,1024]{1,0:T(8,128)(2,1)}, bf16[512,1024]{1,0:T(8,128)(2,1)}, u32[]{:S(2)}, u32[]{:S(2)}) collective-permute-start(bf16[512,1024]{1,0:T(8,128)(2,1)} %get-tuple-element.4), channel_id=1, source_target_pairs={{0,32},{1,97},{2,34},{3,99},{4,36},{5,101},{6,38},{7,103},{8,40},{... | collective-permute-start | bytes 3145736 | tf_op jit(solution)/shard_map/ppermute | solution.py:26
  115.1 38.3 %collective-permute-start.19 = (bf16[512,1024]{1,0:T(8,128)(2,1)}, bf16[512,1024]{1,0:T(8,128)(2,1)}, u32[]{:S(2)}, u32[]{:S(2)}) collective-permute-start(bf16[512,1024]{1,0:T(8,128)(2,1)} %add_convert_fusion), channel_id=1, source_target_pairs={{0,96},{1,33},{2,98},{3,35},{4,100},{5,37},{6,102},{7,39},{8,104},... | collective-permute-start | bytes 3145736 | tf_op jit(solution)/shard_map/ppermute | solution.py:26
  134.2 19.2 %copy-start.11 = (bf16[1024,512]{0,1:T(8,128)(2,1)S(1)}, bf16[1024,512]{0,1:T(8,128)(2,1)}, u32[]{:S(2)}) copy-start(bf16[1024,512]{0,1:T(8,128)(2,1)} %get-tuple-element.17) | copy-start | bytes 3145732
  137.8 15.6 %copy-start.5 = (bf16[512,1024]{1,0:T(8,128)(2,1)S(1)}, bf16[512,1024]{1,0:T(8,128)(2,1)}, u32[]{:S(2)}) copy-start(bf16[512,1024]{1,0:T(8,128)(2,1)} %copy-done.3) | copy-start | bytes 3145732
  137.8 15.6 %copy-start.8 = (bf16[512,1024]{1,0:T(8,128)(2,1)S(1)}, bf16[512,1024]{1,0:T(8,128)(2,1)}, u32[]{:S(2)}) copy-start(bf16[512,1024]{1,0:T(8,128)(2,1)} %copy-done.6) | copy-start | bytes 3145732
  138.0 38.4 %collective-permute-start.11 = (bf16[512,512]{1,0:T(8,128)(2,1)S(1)}, bf16[512,512]{1,0:T(8,128)(2,1)S(1)}, u32[]{:S(2)}, u32[]{:S(2)}) collective-permute-start(bf16[512,512]{1,0:T(8,128)(2,1)S(1)} %get-tuple-element.10), channel_id=1, source_target_pairs={{2,16},{3,17},{6,20},{7,21},{10,24},{11,25},{14,28},{15,29},{16,2}... | collective-permute-start | bytes 1572872 | tf_op jit(solution)/shard_map/ppermute | solution.py:26
  141.3 35.1 %collective-permute-start.12 = (bf16[512,512]{1,0:T(8,128)(2,1)S(1)}, bf16[512,512]{1,0:T(8,128)(2,1)S(1)}, u32[]{:S(2)}, u32[]{:S(2)}) collective-permute-start(bf16[512,512]{1,0:T(8,128)(2,1)S(1)} %get-tuple-element.11), channel_id=1, source_target_pairs={{0,2},{1,3},{2,18},{3,19},{4,6},{5,7},{6,22},{7,23},{8,10},{9,11},... | collective-permute-start | bytes 1572872 | tf_op jit(solution)/shard_map/ppermute | solution.py:26
  156.4 17.5 %copy-start.13 = (f32[512]{0:T(512)S(1)}, f32[512]{0:T(512)}, u32[]{:S(2)}) copy-start(f32[512]{0:T(512)} %param.9) | copy-start | bytes 6148
  156.5 30.5 %collective-permute-start.20 = (bf16[512,512]{1,0:T(8,128)(2,1)S(1)}, bf16[512,512]{1,0:T(8,128)(2,1)S(1)}, u32[]{:S(2)}, u32[]{:S(2)}) collective-permute-start(bf16[512,512]{1,0:T(8,128)(2,1)S(1)} %get-tuple-element.8), channel_id=1, source_target_pairs={{2,16},{3,17},{6,20},{7,21},{10,24},{11,25},{14,28},{15,29},{16,2}... | collective-permute-start | bytes 1572872 | tf_op jit(solution)/shard_map/ppermute | solution.py:26
  159.7 27.2 %collective-permute-start.21 = (bf16[512,512]{1,0:T(8,128)(2,1)S(1)}, bf16[512,512]{1,0:T(8,128)(2,1)S(1)}, u32[]{:S(2)}, u32[]{:S(2)}) collective-permute-start(bf16[512,512]{1,0:T(8,128)(2,1)S(1)} %get-tuple-element.9), channel_id=1, source_target_pairs={{0,2},{1,3},{2,18},{3,19},{4,6},{5,7},{6,22},{7,23},{8,10},{9,11},... | collective-permute-start | bytes 1572872 | tf_op jit(solution)/shard_map/ppermute | solution.py:26
  160.1 3.8 %collective-permute-start.22 = (f32[512]{0:T(512)S(1)}, f32[512]{0:T(512)S(1)}, u32[]{:S(2)}, u32[]{:S(2)}) collective-permute-start(f32[512]{0:T(512)S(1)} %bitcast.49), channel_id=1, source_target_pairs={{0,32},{1,97},{2,34},{3,99},{4,36},{5,101},{6,38},{7,103},{8,40},{... | collective-permute-start | bytes 6152 | tf_op jit(solution)/shard_map/ppermute | solution.py:26
  163.9 2.7 %collective-permute-start.23 = (f32[512]{0:T(512)S(1)}, f32[512]{0:T(512)S(1)}, u32[]{:S(2)}, u32[]{:S(2)}) collective-permute-start(f32[512]{0:T(512)S(1)} %add.93), channel_id=1, source_target_pairs={{0,96},{1,33},{2,98},{3,35},{4,100},{5,37},{6,102},{7,39},{8,104},... | collective-permute-start | bytes 6152 | tf_op jit(solution)/shard_map/ppermute | solution.py:26
  166.6 7.2 %collective-permute-start.24 = (f32[512]{0:T(512)S(1)}, f32[512]{0:T(512)S(1)}, u32[]{:S(2)}, u32[]{:S(2)}) collective-permute-start(f32[512]{0:T(512)S(1)} %add.94), channel_id=1, source_target_pairs={{0,16},{1,17},{2,18},{3,19},{4,20},{5,21},{6,22},{7,23},{8,24},{9,... | collective-permute-start | bytes 6152 | tf_op jit(solution)/shard_map/ppermute | solution.py:26

commit v2 on v1

v2 whole, which is shorter than its diff:
```python
import itertools

import jax
import jax.numpy as jnp
from jax import lax
from jax.sharding import Mesh
from jax.sharding import PartitionSpec as P

AXES = ("z", "l", "x", "h", "c")
SAMP = ("z", "l")
FEAT = ("x", "h", "c")
SIZES = (4, 2, 4, 2, 2)
F32 = jnp.float32
BF16 = jnp.bfloat16


def send(value, route):
    pairs = []
    for source, at in enumerate(itertools.product(*map(range, SIZES))):
        target = route(*at)
        if target is not None:
            index = 0
            for size, place in zip(SIZES, target):
                index = index * size + place % size
            pairs.append((source, index))
    return lax.ppermute(value, AXES, pairs)


def core_swap(value):
    return send(value, lambda z, l, x, h, c: (z, l, x, h, 1 - c))


def other_h(z, l, x, h, c):
    return (z, l, x, 1 - h, c)


def near_route(z, l, x, h, c):
    return (z ^ 1 if c == 0 else 3 - z, l, x, h, c)


def over_route(z, l, x, h, c):
    return (3 - z if c == 0 else z ^ 1, l, x, h, c)


def with_ring(z, l, x, h, c):
    return (z, l, x + 1 - 2 * c, h, c)


def against_ring(z, l, x, h, c):
    return (z, l, x - 1 + 2 * c, h, c)


def sum_over_l(same, other, keeps):
    there = send(other.astype(BF16), lambda z, l, x, h, c: (z, 1 - l, x, 1 - h, c))
    back = send(
        jnp.where(keeps, there, same.astype(BF16)), lambda z, l, x, h, c: (z, 1 - l, x, h, c)
    )
    return jnp.where(keeps, same.astype(F32), there.astype(F32)) + back.astype(F32)


def product(rows, weighted):
    return lax.dot_general(
        rows, weighted, (((0,), (0,)), ((), ())), preferred_element_type=F32
    ).astype(BF16)


def per_device(design, labels, coef_all, active, penalty):
    z, l, x, h, c = (lax.axis_index(name) for name in AXES)
    keeps = l == h
    scale = 1.0 / jnp.sqrt(F32(design.shape[0] * 8))
    half = design.shape[1] // 2

    def halves(array):
        return array[:, :half], array[:, half:]

    mine = [lax.optimization_barrier(half_of) for half_of in halves(design)]
    first = send(design, with_ring)
    far = [send(lax.optimization_barrier(halves(first)[k]), with_ring) for k in range(2)]
    second = [send(mine[k], against_ring) for k in range(2)]
    beside = send(design, other_h)
    across = core_swap(design)
    beta = coef_all[active]
    part = jnp.dot(design, beta.astype(BF16), preferred_element_type=F32)
    part = part + send(part, other_h)
    one = send(part, against_ring)
    two = send(one, against_ring)
    part = part + one + two + send(two, against_ring)
    margin = part + core_swap(part)
    prob = 1.0 / (1.0 + jnp.exp(-margin))
    weight = prob * (1.0 - prob)
    resid_b = (prob - labels.astype(F32)).astype(BF16)
    grad = jnp.dot(resid_b, design, preferred_element_type=F32)
    grad = grad + send(grad, near_route)
    grad = grad + send(grad, over_route)
    grad = grad + send(grad, lambda z, l, x, h, c: (z, 1 - l, x, h, c))
    gradient = grad * scale + penalty * beta

    def weigh(block):
        return (block.astype(F32) * weight[:, None]).astype(BF16)

    first_across = core_swap(first)
    far_across = [core_swap(far[k]) for k in range(2)]
    second_across = [core_swap(second[k]) for k in range(2)]
    places = {
        "q": z ^ 2,
        "p": jnp.where(c == 0, z ^ 1, 3 - z),
        "s": jnp.where(c == 0, 3 - z, z ^ 1),
        "z": z,
    }

    def pick(*block):
        return lax.optimization_barrier(jnp.stack(block))

    def rows_of(k):
        own = pick(mine[k], second[k], far[k], halves(first)[k])
        other = pick(
            halves(across)[k], halves(first_across)[k], far_across[k], second_across[k]
        )
        return own, other

    own, other = [None, None], [None, None]
    own[0], other[0] = rows_of(0)
    beside, own[0], other[0] = lax.optimization_barrier((beside, own[0], other[0]))
    both = jnp.concatenate([weigh(design), weigh(beside)], axis=1)
    both, far[1], second[1] = lax.optimization_barrier((both, far[1], second[1]))
    own[1], other[1] = rows_of(1)

    def products(rows):
        def at(place):
            j = ((place - x) * (1 - 2 * c)) % 4
            return product(lax.dynamic_index_in_dim(rows, j, 0, keepdims=False), both)

        return {name: at(place) for name, place in places.items()}

    def sum_over_z(terms):
        far_side = send(terms["q"].astype(BF16), near_route)
        near_side = send(terms["p"].astype(BF16), near_route)
        passed = terms["s"].astype(F32) + far_side.astype(F32)
        over_side = send(passed.astype(BF16), over_route)
        return terms["z"].astype(F32) + near_side.astype(F32) + over_side.astype(F32)

    width = design.shape[1]
    terms = products(own[0])
    joined = jnp.concatenate(list(terms.values()), axis=0)
    summed = sum_over_l(joined[:, :width], joined[:, width:], keeps)
    blocks = [sum_over_z(dict(zip(terms, jnp.split(summed, 4))))]
    for rows in (other[0], own[1], other[1]):
        total = sum_over_z(products(rows))
        blocks.append(sum_over_l(total[:, :width], total[:, width:], keeps))
    ours = jnp.concatenate([blocks[0], blocks[2]], axis=0) * scale
    theirs = jnp.concatenate([blocks[1], blocks[3]], axis=0) * scale
    top = jnp.where(c == 0, ours, theirs)
    low = jnp.where(c == 0, theirs, ours)
    return (jnp.concatenate([top, low], axis=0), gradient)


def solution(mesh):
    split = Mesh(mesh.devices.reshape(SIZES), AXES)
    placed = (P(SAMP, FEAT), P(SAMP), P(), P(FEAT), P(FEAT))

    return jax.shard_map(
        per_device, mesh=split, in_specs=placed, out_specs=(P(SAMP, FEAT), P(FEAT)), check_vma=False
    )
```

time: 190 us -> 194 us (1.021)
  the two profiles are of different devices: /device:TPU:9 before, /device:TPU:1 now
where the time goes in v2:
time: 194 us
  starting transfers between devices  77.1 us (40%)
  waiting for transfers between devices  73.7 us (38%)
  matrix products  18.4 us (9%)
  local copies, waits for them, and re-layouts  13.7 us (7%)
  other arithmetic  9.87 us (5%)
    ppermute x40, starting transfers between devices, send(): return lax.ppermute(value, AXES, pairs)  77.1 us
    ppermute x40, waiting for transfers between devices, send(): return lax.ppermute(value, AXES, pairs)  73.7 us
    dot_general x16, matrix products, product(): lax.dot_general(rows, weighted, (((0,), (0,)), ((), ())), preferred_eleme...  16.1 us
    gather x1, local copies, waits for them, and re-layouts, per_device(): beta = coef_all[active]  6.5 us
    another operation x3, local copies, waits for them, and re-layouts, pick(): return lax.optimization_barrier(jnp.stack(block))  5.73 us
    another operation x4, other arithmetic, pick(): return lax.optimization_barrier(jnp.stack(block))  4.24 us
  transfers between devices with their start and end apart: 40, of which 21 were waited for; matrix products, arithmetic and copies ran while one was open for 21% of the time, Pallas kernels for 0%

profile of v2, /device:TPU:1, one launch (start us, length us, event | category | flops | bytes accessed | tf_op | source)
XLA Modules:
  0.0 193.9 jit_solution(13357208629266891946)
XLA Ops:
  0.7 3.4 %collective-permute-start.2 = (bf16[1536,512]{1,0:T(8,128)(2,1)}, bf16[1536,512]{1,0:T(8,128)(2,1)}, u32[]{:S(2)}, u32[]{:S(2)}) collective-permute-start(bf16[1536,512]{1,0:T(8,128)(2,1)} %param.5), channel_id=1, source_target_pairs={{0,4},{1,13},{2,6},{3,15},{4,8},{5,1},{6,10},{7,3},{8,12},{9,5},{1... | collective-permute-start | bytes 4718600 | tf_op jit(solution)/shard_map/ppermute | solution.py:26
  4.7 6.5 %gather_fusion = f32[512]{0:T(512)S(1)} fusion(f32[1048576]{0:T(1024)} %param.7, s32[1024]{0:T(1024)S(1)} %pad_clamp_fusion), kind=kCustom, calls=%fused_computation | custom fusion | bytes 6144 | tf_op jit(solution)/shard_map/gather | solution.py:82
  11.2 1.9 convolution_reduce_fusion
  13.2 3.0 %collective-permute-start.8 = (f32[1536]{0:T(1024)S(1)}, f32[1536]{0:T(1024)S(1)}, u32[]{:S(2)}, u32[]{:S(2)}) collective-permute-start(f32[1536]{0:T(1024)S(1)} %convolution_reduce_fusion), channel_id=1, source_target_pairs={{0,2},{1,3},{2,0},{3,1},{4,6},{5,7},{6,4},{7,5},{8,10},{9,11},{10,... | collective-permute-start | bytes 18440 | tf_op jit(solution)/shard_map/ppermute | solution.py:26
  16.2 1.1 collective-permute-done.8
  17.3 4.2 %collective-permute-done.9 = f32[1536]{0:T(1024)S(1)} collective-permute-done((f32[1536]{0:T(1024)S(1)}, f32[1536]{0:T(1024)S(1)}, u32[]{:S(2)}, u32[]{:S(2)}) %collective-permute-start.9) | collective-permute-done | bytes 6176 | tf_op jit(solution)/shard_map/ppermute | solution.py:26
  21.5 3.7 %collective-permute-done.10 = f32[1536]{0:T(1024)S(1)} collective-permute-done((f32[1536]{0:T(1024)S(1)}, f32[1536]{0:T(1024)S(1)}, u32[]{:S(2)}, u32[]{:S(2)}) %collective-permute-start.10) | collective-permute-done | bytes 6176 | tf_op jit(solution)/shard_map/ppermute | solution.py:26
  25.2 3.7 %collective-permute-done.11 = f32[1536]{0:T(1024)S(1)} collective-permute-done((f32[1536]{0:T(1024)S(1)}, f32[1536]{0:T(1024)S(1)}, u32[]{:S(2)}, u32[]{:S(2)}) %collective-permute-start.11) | collective-permute-done | bytes 6176 | tf_op jit(solution)/shard_map/ppermute | solution.py:26
  28.9 2.1 %collective-permute-start.12 = (f32[1536]{0:T(1024)S(1)}, f32[1536]{0:T(1024)S(1)}, u32[]{:S(2)}, u32[]{:S(2)}) collective-permute-start(f32[1536]{0:T(1024)S(1)} %add_add_fusion), channel_id=1, source_target_pairs={{0,1},{1,0},{2,3},{3,2},{4,5},{5,4},{6,7},{7,6},{8,9},{9,8},{10,11... | collective-permute-start | bytes 18440 | tf_op jit(solution)/shard_map/ppermute | solution.py:26
  32.1 3.8 %collective-permute-start.37 = (f32[512]{0:T(512)S(1)}, f32[512]{0:T(512)S(1)}, u32[]{:S(2)}, u32[]{:S(2)}) collective-permute-start(f32[512]{0:T(512)S(1)} %bitcast.96), channel_id=1, source_target_pairs={{0,32},{1,97},{2,34},{3,99},{4,36},{5,101},{6,38},{7,103},{8,40},{... | collective-permute-start | bytes 6152 | tf_op jit(solution)/shard_map/ppermute | solution.py:26
  37.0 1.2 fusion.74
  38.2 1.1 collective-permute-start.14
  39.4 1.3 collective-permute-start.39
  40.7 5.9 %collective-permute-start.5 = (bf16[1536,512]{1,0:T(8,128)(2,1)}, bf16[1536,512]{1,0:T(8,128)(2,1)}, u32[]{:S(2)}, u32[]{:S(2)}) collective-permute-start(bf16[1536,512]{1,0:T(8,128)(2,1)} %collective-permute-done.2), channel_id=1, source_target_pairs={{0,1},{1,0},{2,3},{3,2},{4,5},{5,4},{6,7},{7,6},{8,9},{9,8},{10,11... | collective-permute-start | bytes 4718600 | tf_op jit(solution)/shard_map/ppermute | solution.py:26
  46.6 2.8 %slice_bitcast_fusion.4 = (bf16[1,1536,256]{2,1,0:T(8,128)(2,1)S(1)}, bf16[1,1536,256]{2,1,0:T(8,128)(2,1)S(1)}, bf16[1536,256]{1,0:T(8,128)(2,1)}, bf16[1536,256]{1,0:T(8,128)(2,1)}) fusion(bf16[1536,512]{1,0:T(8,128)(2,1)} %collective-permute-done.2), kind=kLoop, calls=%fused_computation.126 | loop fusion | bytes 4718592 | tf_op jit(solution)/shard_map/stack | solution.py:112
  50.0 1.1 collective-permute-done.1
  51.1 2.9 %collective-permute-start = (bf16[1536,512]{1,0:T(8,128)(2,1)S(1)}, bf16[1536,512]{1,0:T(8,128)(2,1)S(1)}, u32[]{:S(2)}, u32[]{:S(2)}) collective-permute-start(bf16[1536,512]{1,0:T(8,128)(2,1)S(1)} %copy-done), channel_id=1, source_target_pairs={{0,2},{1,3},{2,0},{3,1},{4,6},{5,7},{6,4},{7,5},{8,10},{9,11},{10,... | collective-permute-start | bytes 4718600 | tf_op jit(solution)/shard_map/ppermute | solution.py:26
  54.0 2.1 %collective-permute-start.13 = (bf16[1536,256]{1,0:T(8,128)(2,1)}, bf16[1536,256]{1,0:T(8,128)(2,1)S(1)}, u32[]{:S(2)}, u32[]{:S(2)}) collective-permute-start(bf16[1536,256]{1,0:T(8,128)(2,1)} %get-tuple-element.20), channel_id=1, source_target_pairs={{0,4},{1,13},{2,6},{3,15},{4,8},{5,1},{6,10},{7,3},{8,12},{9,5},{1... | collective-permute-start | bytes 2359304 | tf_op jit(solution)/shard_map/ppermute | solution.py:26
  56.1 1.5 slice_bitcast_fusion.1
  57.6 8.0 %collective-permute-done.14 = bf16[1536,256]{1,0:T(8,128)(2,1)} collective-permute-done((bf16[1536,256]{1,0:T(8,128)(2,1)}, bf16[1536,256]{1,0:T(8,128)(2,1)}, u32[]{:S(2)}, u32[]{:S(2)}) %collective-permute-start.14) | collective-permute-done | bytes 786464 | tf_op jit(solution)/shard_map/ppermute | solution.py:26
  65.6 10.2 %collective-permute-start.7 = (bf16[1536,256]{1,0:T(8,128)(2,1)}, bf16[1536,256]{1,0:T(8,128)(2,1)S(1)}, u32[]{:S(2)}, u32[]{:S(2)}) collective-permute-start(bf16[1536,256]{1,0:T(8,128)(2,1)} %collective-permute-done.1), channel_id=1, source_target_pairs={{0,1},{1,0},{2,3},{3,2},{4,5},{5,4},{6,7},{7,6},{8,9},{9,8},{10,11... | collective-permute-start | bytes 2359304 | tf_op jit(solution)/shard_map/ppermute | solution.py:26
  75.7 1.8 pad_maximum_fusion
  77.6 2.1 %collective-permute-done.13 = bf16[1536,256]{1,0:T(8,128)(2,1)S(1)} collective-permute-done((bf16[1536,256]{1,0:T(8,128)(2,1)}, bf16[1536,256]{1,0:T(8,128)(2,1)S(1)}, u32[]{:S(2)}, u32[]{:S(2)}) %collective-permute-start.13) | collective-permute-done | bytes 786464 | tf_op jit(solution)/shard_map/ppermute | solution.py:26
  80.1 1.5 slice_bitcast_fusion
  85.2 1.6 pad_maximum_fusion.3
  91.2 2.8 %collective-permute-start.15 = (bf16[1024,512]{1,0:T(8,128)(2,1)S(1)}, bf16[1024,512]{1,0:T(8,128)(2,1)S(1)}, u32[]{:S(2)}, u32[]{:S(2)}) collective-permute-start(bf16[1024,512]{1,0:T(8,128)(2,1)S(1)} %slice.76), channel_id=1, source_target_pairs={{0,18},{1,19},{2,16},{3,17},{4,22},{5,23},{6,20},{7,21},{8,26},{9,... | collective-permute-start | bytes 3145736 | tf_op jit(solution)/shard_map/ppermute | solution.py:26
  94.0 8.9 %collective-permute-start.20 = (bf16[256,1024]{1,0:T(8,128)(2,1)S(1)}, bf16[256,1024]{1,0:T(8,128)(2,1)S(1)}, u32[]{:S(2)}, u32[]{:S(2)}) collective-permute-start(bf16[256,1024]{1,0:T(8,128)(2,1)S(1)} %convolution_convert_fusion.10), channel_id=1, source_target_pairs={{0,32},{1,97},{2,34},{3,99},{4,36},{5,101},{6,38},{7,103},{8,40},{... | collective-permute-start | bytes 1572872 | tf_op jit(solution)/shard_map/ppermute | solution.py:26
  104.9 2.7 %collective-permute-start.25 = (bf16[256,1024]{1,0:T(8,128)(2,1)S(1)}, bf16[256,1024]{1,0:T(8,128)(2,1)S(1)}, u32[]{:S(2)}, u32[]{:S(2)}) collective-permute-start(bf16[256,1024]{1,0:T(8,128)(2,1)S(1)} %convolution_convert_fusion.6), channel_id=1, source_target_pairs={{0,32},{1,97},{2,34},{3,99},{4,36},{5,101},{6,38},{7,103},{8,40},{... | collective-permute-start | bytes 1572872 | tf_op jit(solution)/shard_map/ppermute | solution.py:26
  110.2 5.1 %collective-permute-done.21 = bf16[256,1024]{1,0:T(8,128)(2,1)S(1)} collective-permute-done((bf16[256,1024]{1,0:T(8,128)(2,1)S(1)}, bf16[256,1024]{1,0:T(8,128)(2,1)S(1)}, u32[]{:S(2)}, u32[]{:S(2)}) %collective-permute-start.21) | collective-permute-done | bytes 524320 | tf_op jit(solution)/shard_map/ppermute | solution.py:26
  115.3 2.7 %collective-permute-start.33 = (bf16[256,1024]{1,0:T(8,128)(2,1)S(1)}, bf16[256,1024]{1,0:T(8,128)(2,1)S(1)}, u32[]{:S(2)}, u32[]{:S(2)}) collective-permute-start(bf16[256,1024]{1,0:T(8,128)(2,1)S(1)} %convolution_convert_fusion), channel_id=1, source_target_pairs={{0,32},{1,97},{2,34},{3,99},{4,36},{5,101},{6,38},{7,103},{8,40},{... | collective-permute-start | bytes 1572872 | tf_op jit(solution)/shard_map/ppermute | solution.py:26
  119.0 7.3 %collective-permute-done.26 = bf16[256,1024]{1,0:T(8,128)(2,1)S(1)} collective-permute-done((bf16[256,1024]{1,0:T(8,128)(2,1)S(1)}, bf16[256,1024]{1,0:T(8,128)(2,1)S(1)}, u32[]{:S(2)}, u32[]{:S(2)}) %collective-permute-start.26) | collective-permute-done | bytes 524320 | tf_op jit(solution)/shard_map/ppermute | solution.py:26
  126.3 2.7 %collective-permute-start.32 = (bf16[256,1024]{1,0:T(8,128)(2,1)S(1)}, bf16[256,1024]{1,0:T(8,128)(2,1)S(1)}, u32[]{:S(2)}, u32[]{:S(2)}) collective-permute-start(bf16[256,1024]{1,0:T(8,128)(2,1)S(1)} %convolution_convert_fusion.2), channel_id=1, source_target_pairs={{0,32},{1,97},{2,34},{3,99},{4,36},{5,101},{6,38},{7,103},{8,40},{... | collective-permute-start | bytes 1572872 | tf_op jit(solution)/shard_map/ppermute | solution.py:26
  129.0 1.0 fusion.8
  130.0 1.9 collective-permute-done.33
  131.9 4.0 %collective-permute-start.22 = (bf16[256,1024]{1,0:T(8,128)(2,1)S(1)}, bf16[256,1024]{1,0:T(8,128)(2,1)S(1)}, u32[]{:S(2)}, u32[]{:S(2)}) collective-permute-start(bf16[256,1024]{1,0:T(8,128)(2,1)S(1)} %fusion.14), channel_id=1, source_target_pairs={{0,96},{1,33},{2,98},{3,35},{4,100},{5,37},{6,102},{7,39},{8,104},... | collective-permute-start | bytes 1572872 | tf_op jit(solution)/shard_map/ppermute | solution.py:26
  137.1 1.5 collective-permute-start.34
  138.7 5.5 %collective-permute-done.22 = bf16[256,1024]{1,0:T(8,128)(2,1)S(1)} collective-permute-done((bf16[256,1024]{1,0:T(8,128)(2,1)S(1)}, bf16[256,1024]{1,0:T(8,128)(2,1)S(1)}, u32[]{:S(2)}, u32[]{:S(2)}) %collective-permute-start.22) | collective-permute-done | bytes 524320 | tf_op jit(solution)/shard_map/ppermute | solution.py:26
  145.9 3.8 %collective-permute-done.27 = bf16[256,1024]{1,0:T(8,128)(2,1)S(1)} collective-permute-done((bf16[256,1024]{1,0:T(8,128)(2,1)S(1)}, bf16[256,1024]{1,0:T(8,128)(2,1)S(1)}, u32[]{:S(2)}, u32[]{:S(2)}) %collective-permute-start.27) | collective-permute-done | bytes 524320 | tf_op jit(solution)/shard_map/ppermute | solution.py:26
  150.9 4.5 %collective-permute-done.34 = bf16[256,1024]{1,0:T(8,128)(2,1)S(1)} collective-permute-done((bf16[256,1024]{1,0:T(8,128)(2,1)S(1)}, bf16[256,1024]{1,0:T(8,128)(2,1)S(1)}, u32[]{:S(2)}, u32[]{:S(2)}) %collective-permute-start.34) | collective-permute-done | bytes 524320 | tf_op jit(solution)/shard_map/ppermute | solution.py:26
  156.7 1.8 collective-permute-done.28
  159.2 4.9 %collective-permute-done.35 = bf16[256,512]{1,0:T(8,128)(2,1)S(1)} collective-permute-done((bf16[256,512]{1,0:T(8,128)(2,1)S(1)}, bf16[256,512]{1,0:T(8,128)(2,1)S(1)}, u32[]{:S(2)}, u32[]{:S(2)}) %collective-permute-start.35) | collective-permute-done | bytes 262176 | tf_op jit(solution)/shard_map/ppermute | solution.py:26
  164.8 8.2 %collective-permute-done.24 = bf16[256,512]{1,0:T(8,128)(2,1)S(1)} collective-permute-done((bf16[256,512]{1,0:T(8,128)(2,1)S(1)}, bf16[256,512]{1,0:T(8,128)(2,1)S(1)}, u32[]{:S(2)}, u32[]{:S(2)}) %collective-permute-start.24) | collective-permute-done | bytes 262176 | tf_op jit(solution)/shard_map/ppermute | solution.py:26
  173.7 6.9 %collective-permute-start.18 = (bf16[256,512]{1,0:T(8,128)(2,1)S(1)}, bf16[256,512]{1,0:T(8,128)(2,1)S(1)}, u32[]{:S(2)}, u32[]{:S(2)}) collective-permute-start(bf16[256,512]{1,0:T(8,128)(2,1)S(1)} %get-tuple-element.29), channel_id=1, source_target_pairs={{0,32},{1,97},{2,34},{3,99},{4,36},{5,101},{6,38},{7,103},{8,40},{... | collective-permute-start | bytes 786440 | tf_op jit(solution)/shard_map/ppermute | solution.py:26
  180.8 4.9 %collective-permute-start.17 = (bf16[256,512]{1,0:T(8,128)(2,1)S(1)}, bf16[256,512]{1,0:T(8,128)(2,1)S(1)}, u32[]{:S(2)}, u32[]{:S(2)}) collective-permute-start(bf16[256,512]{1,0:T(8,128)(2,1)S(1)} %get-tuple-element.28), channel_id=1, source_target_pairs={{0,32},{1,97},{2,34},{3,99},{4,36},{5,101},{6,38},{7,103},{8,40},{... | collective-permute-start | bytes 786440 | tf_op jit(solution)/shard_map/ppermute | solution.py:26
  185.7 1.2 collective-permute-start.19
  187.0 2.3 %collective-permute-done.17 = bf16[256,512]{1,0:T(8,128)(2,1)S(1)} collective-permute-done((bf16[256,512]{1,0:T(8,128)(2,1)S(1)}, bf16[256,512]{1,0:T(8,128)(2,1)S(1)}, u32[]{:S(2)}, u32[]{:S(2)}) %collective-permute-start.17) | collective-permute-done | bytes 262176 | tf_op jit(solution)/shard_map/ppermute | solution.py:26
  189.4 2.6 %collective-permute-done.19 = bf16[256,512]{1,0:T(8,128)(2,1)S(1)} collective-permute-done((bf16[256,512]{1,0:T(8,128)(2,1)S(1)}, bf16[256,512]{1,0:T(8,128)(2,1)S(1)}, u32[]{:S(2)}, u32[]{:S(2)}) %collective-permute-start.19) | collective-permute-done | bytes 262176 | tf_op jit(solution)/shard_map/ppermute | solution.py:26
  192.4 1.5 pad_maximum_fusion.6
  (96 shorter events, 25.6 us)
Async XLA Ops:
  0.6 30.3 %copy-start = (bf16[1536,512]{1,0:T(8,128)(2,1)S(1)}, bf16[1536,512]{1,0:T(8,128)(2,1)}, u32[]{:S(2)}) copy-start(bf16[1536,512]{1,0:T(8,128)(2,1)} %param.5) | copy-start | bytes 4718596
  0.6 31.2 %copy-start.1 = (s32[1536]{0:T(1024)S(1)}, s32[1536]{0:T(1024)}, u32[]{:S(2)}) copy-start(s32[1536]{0:T(1024)} %param.6) | copy-start | bytes 18436
  0.7 40.0 %collective-permute-start.2 = (bf16[1536,512]{1,0:T(8,128)(2,1)}, bf16[1536,512]{1,0:T(8,128)(2,1)}, u32[]{:S(2)}, u32[]{:S(2)}) collective-permute-start(bf16[1536,512]{1,0:T(8,128)(2,1)} %param.5), channel_id=1, source_target_pairs={{0,4},{1,13},{2,6},{3,15},{4,8},{5,1},{6,10},{7,3},{8,12},{9,5},{1... | collective-permute-start | bytes 4718600 | tf_op jit(solution)/shard_map/ppermute | solution.py:26
  13.2 4.1 %collective-permute-start.8 = (f32[1536]{0:T(1024)S(1)}, f32[1536]{0:T(1024)S(1)}, u32[]{:S(2)}, u32[]{:S(2)}) collective-permute-start(f32[1536]{0:T(1024)S(1)} %convolution_reduce_fusion), channel_id=1, source_target_pairs={{0,2},{1,3},{2,0},{3,1},{4,6},{5,7},{6,4},{7,5},{8,10},{9,11},{10,... | collective-permute-start | bytes 18440 | tf_op jit(solution)/shard_map/ppermute | solution.py:26
  17.3 4.2 %collective-permute-start.9 = (f32[1536]{0:T(1024)S(1)}, f32[1536]{0:T(1024)S(1)}, u32[]{:S(2)}, u32[]{:S(2)}) collective-permute-start(f32[1536]{0:T(1024)S(1)} %add.138), channel_id=1, source_target_pairs={{0,12},{1,5},{2,14},{3,7},{4,0},{5,9},{6,2},{7,11},{8,4},{9,13},{1... | collective-permute-start | bytes 18440 | tf_op jit(solution)/shard_map/ppermute | solution.py:26
  21.5 3.7 %collective-permute-start.10 = (f32[1536]{0:T(1024)S(1)}, f32[1536]{0:T(1024)S(1)}, u32[]{:S(2)}, u32[]{:S(2)}) collective-permute-start(f32[1536]{0:T(1024)S(1)} %collective-permute-done.9), channel_id=1, source_target_pairs={{0,12},{1,5},{2,14},{3,7},{4,0},{5,9},{6,2},{7,11},{8,4},{9,13},{1... | collective-permute-start | bytes 18440 | tf_op jit(solution)/shard_map/ppermute | solution.py:26
  25.2 3.7 %collective-permute-start.11 = (f32[1536]{0:T(1024)S(1)}, f32[1536]{0:T(1024)S(1)}, u32[]{:S(2)}, u32[]{:S(2)}) collective-permute-start(f32[1536]{0:T(1024)S(1)} %collective-permute-done.10), channel_id=1, source_target_pairs={{0,12},{1,5},{2,14},{3,7},{4,0},{5,9},{6,2},{7,11},{8,4},{9,13},{1... | collective-permute-start | bytes 18440 | tf_op jit(solution)/shard_map/ppermute | solution.py:26
  28.9 2.9 %collective-permute-start.12 = (f32[1536]{0:T(1024)S(1)}, f32[1536]{0:T(1024)S(1)}, u32[]{:S(2)}, u32[]{:S(2)}) collective-permute-start(f32[1536]{0:T(1024)S(1)} %add_add_fusion), channel_id=1, source_target_pairs={{0,1},{1,0},{2,3},{3,2},{4,5},{5,4},{6,7},{7,6},{8,9},{9,8},{10,11... | collective-permute-start | bytes 18440 | tf_op jit(solution)/shard_map/ppermute | solution.py:26
  31.0 23.1 %collective-permute-start.4 = (bf16[1536,512]{1,0:T(8,128)(2,1)S(1)}, bf16[1536,512]{1,0:T(8,128)(2,1)}, u32[]{:S(2)}, u32[]{:S(2)}) collective-permute-start(bf16[1536,512]{1,0:T(8,128)(2,1)S(1)} %copy-done), channel_id=1, source_target_pairs={{0,1},{1,0},{2,3},{3,2},{4,5},{5,4},{6,7},{7,6},{8,9},{9,8},{10,11... | collective-permute-start | bytes 4718600 | tf_op jit(solution)/shard_map/ppermute | solution.py:26
  32.1 4.8 %collective-permute-start.37 = (f32[512]{0:T(512)S(1)}, f32[512]{0:T(512)S(1)}, u32[]{:S(2)}, u32[]{:S(2)}) collective-permute-start(f32[512]{0:T(512)S(1)} %bitcast.96), channel_id=1, source_target_pairs={{0,32},{1,97},{2,34},{3,99},{4,36},{5,101},{6,38},{7,103},{8,40},{... | collective-permute-start | bytes 6152 | tf_op jit(solution)/shard_map/ppermute | solution.py:26
  37.0 2.4 %collective-permute-start.38 = (f32[512]{0:T(512)S(1)}, f32[512]{0:T(512)S(1)}, u32[]{:S(2)}, u32[]{:S(2)}) collective-permute-start(f32[512]{0:T(512)S(1)} %add.166), channel_id=1, source_target_pairs={{0,96},{1,33},{2,98},{3,35},{4,100},{5,37},{6,102},{7,39},{8,104},... | collective-permute-start | bytes 6152 | tf_op jit(solution)/shard_map/ppermute | solution.py:26
  38.2 11.2 %copy-start.2 = (f32[512]{0:T(512)S(1)}, f32[512]{0:T(512)}, u32[]{:S(2)}) copy-start(f32[512]{0:T(512)} %param.9) | copy-start | bytes 6148
  38.2 12.9 %collective-permute-start.1 = (bf16[1536,256]{1,0:T(8,128)(2,1)}, bf16[1536,256]{1,0:T(8,128)(2,1)}, u32[]{:S(2)}, u32[]{:S(2)}) collective-permute-start(bf16[1536,256]{1,0:T(8,128)(2,1)} %get-tuple-element.27), channel_id=1, source_target_pairs={{0,12},{1,5},{2,14},{3,7},{4,0},{5,9},{6,2},{7,11},{8,4},{9,13},{1... | collective-permute-start | bytes 2359304 | tf_op jit(solution)/shard_map/ppermute | solution.py:26
  38.2 27.4 %collective-permute-start.14 = (bf16[1536,256]{1,0:T(8,128)(2,1)}, bf16[1536,256]{1,0:T(8,128)(2,1)}, u32[]{:S(2)}, u32[]{:S(2)}) collective-permute-start(bf16[1536,256]{1,0:T(8,128)(2,1)} %get-tuple-element.26), channel_id=1, source_target_pairs={{0,12},{1,5},{2,14},{3,7},{4,0},{5,9},{6,2},{7,11},{8,4},{9,13},{1... | collective-permute-start | bytes 2359304 | tf_op jit(solution)/shard_map/ppermute | solution.py:26
  39.4 10.0 %collective-permute-start.39 = (f32[512]{0:T(512)S(1)}, f32[512]{0:T(512)S(1)}, u32[]{:S(2)}, u32[]{:S(2)}) collective-permute-start(f32[512]{0:T(512)S(1)} %add.167), channel_id=1, source_target_pairs={{0,16},{1,17},{2,18},{3,19},{4,20},{5,21},{6,22},{7,23},{8,24},{9,... | collective-permute-start | bytes 6152 | tf_op jit(solution)/shard_map/ppermute | solution.py:26
  40.7 38.9 %collective-permute-start.5 = (bf16[1536,512]{1,0:T(8,128)(2,1)}, bf16[1536,512]{1,0:T(8,128)(2,1)}, u32[]{:S(2)}, u32[]{:S(2)}) collective-permute-start(bf16[1536,512]{1,0:T(8,128)(2,1)} %collective-permute-done.2), channel_id=1, source_target_pairs={{0,1},{1,0},{2,3},{3,2},{4,5},{5,4},{6,7},{7,6},{8,9},{9,8},{10,11... | collective-permute-start | bytes 4718600 | tf_op jit(solution)/shard_map/ppermute | solution.py:26
  49.4 26.3 %collective-permute-start.3 = (bf16[1536,256]{1,0:T(8,128)(2,1)}, bf16[1536,256]{1,0:T(8,128)(2,1)}, u32[]{:S(2)}, u32[]{:S(2)}) collective-permute-start(bf16[1536,256]{1,0:T(8,128)(2,1)} %get-tuple-element.21), channel_id=1, source_target_pairs={{0,4},{1,13},{2,6},{3,15},{4,8},{5,1},{6,10},{7,3},{8,12},{9,5},{1... | collective-permute-start | bytes 2359304 | tf_op jit(solution)/shard_map/ppermute | solution.py:26
  51.1 31.0 %collective-permute-start = (bf16[1536,512]{1,0:T(8,128)(2,1)S(1)}, bf16[1536,512]{1,0:T(8,128)(2,1)S(1)}, u32[]{:S(2)}, u32[]{:S(2)}) collective-permute-start(bf16[1536,512]{1,0:T(8,128)(2,1)S(1)} %copy-done), channel_id=1, source_target_pairs={{0,2},{1,3},{2,0},{3,1},{4,6},{5,7},{6,4},{7,5},{8,10},{9,11},{10,... | collective-permute-start | bytes 4718600 | tf_op jit(solution)/shard_map/ppermute | solution.py:26
  54.0 25.6 %collective-permute-start.13 = (bf16[1536,256]{1,0:T(8,128)(2,1)}, bf16[1536,256]{1,0:T(8,128)(2,1)S(1)}, u32[]{:S(2)}, u32[]{:S(2)}) collective-permute-start(bf16[1536,256]{1,0:T(8,128)(2,1)} %get-tuple-element.20), channel_id=1, source_target_pairs={{0,4},{1,13},{2,6},{3,15},{4,8},{5,1},{6,10},{7,3},{8,12},{9,5},{1... | collective-permute-start | bytes 2359304 | tf_op jit(solution)/shard_map/ppermute | solution.py:26
  65.6 16.1 %collective-permute-start.7 = (bf16[1536,256]{1,0:T(8,128)(2,1)}, bf16[1536,256]{1,0:T(8,128)(2,1)S(1)}, u32[]{:S(2)}, u32[]{:S(2)}) collective-permute-start(bf16[1536,256]{1,0:T(8,128)(2,1)} %collective-permute-done.1), channel_id=1, source_target_pairs={{0,1},{1,0},{2,3},{3,2},{4,5},{5,4},{6,7},{7,6},{8,9},{9,8},{10,11... | collective-permute-start | bytes 2359304 | tf_op jit(solution)/shard_map/ppermute | solution.py:26
  75.7 5.9 %collective-permute-start.6 = (bf16[1536,256]{1,0:T(8,128)(2,1)}, bf16[1536,256]{1,0:T(8,128)(2,1)S(1)}, u32[]{:S(2)}, u32[]{:S(2)}) collective-permute-start(bf16[1536,256]{1,0:T(8,128)(2,1)} %collective-permute-done.3), channel_id=1, source_target_pairs={{0,1},{1,0},{2,3},{3,2},{4,5},{5,4},{6,7},{7,6},{8,9},{9,8},{10,11... | collective-permute-start | bytes 2359304 | tf_op jit(solution)/shard_map/ppermute | solution.py:26
  79.6 25.3 %collective-permute-start.31 = (bf16[1536,256]{1,0:T(8,128)(2,1)}, bf16[1536,256]{1,0:T(8,128)(2,1)S(1)}, u32[]{:S(2)}, u32[]{:S(2)}) collective-permute-start(bf16[1536,256]{1,0:T(8,128)(2,1)} %collective-permute-done.14), channel_id=1, source_target_pairs={{0,1},{1,0},{2,3},{3,2},{4,5},{5,4},{6,7},{7,6},{8,9},{9,8},{10,11... | collective-permute-start | bytes 2359304 | tf_op jit(solution)/shard_map/ppermute | solution.py:26
  79.6 28.0 %collective-permute-start.30 = (bf16[1536,256]{1,0:T(8,128)(2,1)S(1)}, bf16[1536,256]{1,0:T(8,128)(2,1)S(1)}, u32[]{:S(2)}, u32[]{:S(2)}) collective-permute-start(bf16[1536,256]{1,0:T(8,128)(2,1)S(1)} %collective-permute-done.13), channel_id=1, source_target_pairs={{0,1},{1,0},{2,3},{3,2},{4,5},{5,4},{6,7},{7,6},{8,9},{9,8},{10,11... | collective-permute-start | bytes 2359304 | tf_op jit(solution)/shard_map/ppermute | solution.py:26
  91.2 45.7 %collective-permute-start.15 = (bf16[1024,512]{1,0:T(8,128)(2,1)S(1)}, bf16[1024,512]{1,0:T(8,128)(2,1)S(1)}, u32[]{:S(2)}, u32[]{:S(2)}) collective-permute-start(bf16[1024,512]{1,0:T(8,128)(2,1)S(1)} %slice.76), channel_id=1, source_target_pairs={{0,18},{1,19},{2,16},{3,17},{4,22},{5,23},{6,20},{7,21},{8,26},{9,... | collective-permute-start | bytes 3145736 | tf_op jit(solution)/shard_map/ppermute | solution.py:26
  94.0 43.1 %collective-permute-start.20 = (bf16[256,1024]{1,0:T(8,128)(2,1)S(1)}, bf16[256,1024]{1,0:T(8,128)(2,1)S(1)}, u32[]{:S(2)}, u32[]{:S(2)}) collective-permute-start(bf16[256,1024]{1,0:T(8,128)(2,1)S(1)} %convolution_convert_fusion.10), channel_id=1, source_target_pairs={{0,32},{1,97},{2,34},{3,99},{4,36},{5,101},{6,38},{7,103},{8,40},{... | collective-permute-start | bytes 1572872 | tf_op jit(solution)/shard_map/ppermute | solution.py:26
  102.9 12.5 %collective-permute-start.21 = (bf16[256,1024]{1,0:T(8,128)(2,1)S(1)}, bf16[256,1024]{1,0:T(8,128)(2,1)S(1)}, u32[]{:S(2)}, u32[]{:S(2)}) collective-permute-start(bf16[256,1024]{1,0:T(8,128)(2,1)S(1)} %convolution_convert_fusion.8), channel_id=1, source_target_pairs={{0,32},{1,97},{2,34},{3,99},{4,36},{5,101},{6,38},{7,103},{8,40},{... | collective-permute-start | bytes 1572872 | tf_op jit(solution)/shard_map/ppermute | solution.py:26
  104.9 40.3 %collective-permute-start.25 = (bf16[256,1024]{1,0:T(8,128)(2,1)S(1)}, bf16[256,1024]{1,0:T(8,128)(2,1)S(1)}, u32[]{:S(2)}, u32[]{:S(2)}) collective-permute-start(bf16[256,1024]{1,0:T(8,128)(2,1)S(1)} %convolution_convert_fusion.6), channel_id=1, source_target_pairs={{0,32},{1,97},{2,34},{3,99},{4,36},{5,101},{6,38},{7,103},{8,40},{... | collective-permute-start | bytes 1572872 | tf_op jit(solution)/shard_map/ppermute | solution.py:26
  107.7 18.6 %collective-permute-start.26 = (bf16[256,1024]{1,0:T(8,128)(2,1)S(1)}, bf16[256,1024]{1,0:T(8,128)(2,1)S(1)}, u32[]{:S(2)}, u32[]{:S(2)}) collective-permute-start(bf16[256,1024]{1,0:T(8,128)(2,1)S(1)} %convolution_convert_fusion.4), channel_id=1, source_target_pairs={{0,32},{1,97},{2,34},{3,99},{4,36},{5,101},{6,38},{7,103},{8,40},{... | collective-permute-start | bytes 1572872 | tf_op jit(solution)/shard_map/ppermute | solution.py:26
  115.3 16.6 %collective-permute-start.33 = (bf16[256,1024]{1,0:T(8,128)(2,1)S(1)}, bf16[256,1024]{1,0:T(8,128)(2,1)S(1)}, u32[]{:S(2)}, u32[]{:S(2)}) collective-permute-start(bf16[256,1024]{1,0:T(8,128)(2,1)S(1)} %convolution_convert_fusion), channel_id=1, source_target_pairs={{0,32},{1,97},{2,34},{3,99},{4,36},{5,101},{6,38},{7,103},{8,40},{... | collective-permute-start | bytes 1572872 | tf_op jit(solution)/shard_map/ppermute | solution.py:26
  126.3 24.6 %collective-permute-start.32 = (bf16[256,1024]{1,0:T(8,128)(2,1)S(1)}, bf16[256,1024]{1,0:T(8,128)(2,1)S(1)}, u32[]{:S(2)}, u32[]{:S(2)}) collective-permute-start(bf16[256,1024]{1,0:T(8,128)(2,1)S(1)} %convolution_convert_fusion.2), channel_id=1, source_target_pairs={{0,32},{1,97},{2,34},{3,99},{4,36},{5,101},{6,38},{7,103},{8,40},{... | collective-permute-start | bytes 1572872 | tf_op jit(solution)/shard_map/ppermute | solution.py:26
  131.9 12.2 %collective-permute-start.22 = (bf16[256,1024]{1,0:T(8,128)(2,1)S(1)}, bf16[256,1024]{1,0:T(8,128)(2,1)S(1)}, u32[]{:S(2)}, u32[]{:S(2)}) collective-permute-start(bf16[256,1024]{1,0:T(8,128)(2,1)S(1)} %fusion.14), channel_id=1, source_target_pairs={{0,96},{1,33},{2,98},{3,35},{4,100},{5,37},{6,102},{7,39},{8,104},... | collective-permute-start | bytes 1572872 | tf_op jit(solution)/shard_map/ppermute | solution.py:26
  136.9 12.8 %collective-permute-start.27 = (bf16[256,1024]{1,0:T(8,128)(2,1)S(1)}, bf16[256,1024]{1,0:T(8,128)(2,1)S(1)}, u32[]{:S(2)}, u32[]{:S(2)}) collective-permute-start(bf16[256,1024]{1,0:T(8,128)(2,1)S(1)} %fusion.8), channel_id=1, source_target_pairs={{0,96},{1,33},{2,98},{3,35},{4,100},{5,37},{6,102},{7,39},{8,104},... | collective-permute-start | bytes 1572872 | tf_op jit(solution)/shard_map/ppermute | solution.py:26
  137.1 18.2 %collective-permute-start.34 = (bf16[256,1024]{1,0:T(8,128)(2,1)S(1)}, bf16[256,1024]{1,0:T(8,128)(2,1)S(1)}, u32[]{:S(2)}, u32[]{:S(2)}) collective-permute-start(bf16[256,1024]{1,0:T(8,128)(2,1)S(1)} %fusion.2), channel_id=1, source_target_pairs={{0,96},{1,33},{2,98},{3,35},{4,100},{5,37},{6,102},{7,39},{8,104},... | collective-permute-start | bytes 1572872 | tf_op jit(solution)/shard_map/ppermute | solution.py:26
  144.1 28.9 %collective-permute-start.16 = (bf16[1024,512]{1,0:T(8,128)(2,1)S(1)}, bf16[1024,512]{1,0:T(8,128)(2,1)S(1)}, u32[]{:S(2)}, u32[]{:S(2)}) collective-permute-start(bf16[1024,512]{1,0:T(8,128)(2,1)S(1)} %broadcast_select_fusion), channel_id=1, source_target_pairs={{0,16},{1,17},{2,18},{3,19},{4,20},{5,21},{6,22},{7,23},{8,24},{9,... | collective-permute-start | bytes 3145736 | tf_op jit(solution)/shard_map/ppermute | solution.py:26
  145.2 11.3 %collective-permute-start.23 = (bf16[256,512]{1,0:T(8,128)(2,1)S(1)}, bf16[256,512]{1,0:T(8,128)(2,1)S(1)}, u32[]{:S(2)}, u32[]{:S(2)}) collective-permute-start(bf16[256,512]{1,0:T(8,128)(2,1)S(1)} %slice.110), channel_id=1, source_target_pairs={{0,18},{1,19},{2,16},{3,17},{4,22},{5,23},{6,20},{7,21},{8,26},{9,... | collective-permute-start | bytes 786440 | tf_op jit(solution)/shard_map/ppermute | solution.py:26
  150.8 7.7 %collective-permute-start.28 = (bf16[256,512]{1,0:T(8,128)(2,1)S(1)}, bf16[256,512]{1,0:T(8,128)(2,1)S(1)}, u32[]{:S(2)}, u32[]{:S(2)}) collective-permute-start(bf16[256,512]{1,0:T(8,128)(2,1)S(1)} %slice.109), channel_id=1, source_target_pairs={{0,18},{1,19},{2,16},{3,17},{4,22},{5,23},{6,20},{7,21},{8,26},{9,... | collective-permute-start | bytes 786440 | tf_op jit(solution)/shard_map/ppermute | solution.py:26
  156.4 7.7 %collective-permute-start.35 = (bf16[256,512]{1,0:T(8,128)(2,1)S(1)}, bf16[256,512]{1,0:T(8,128)(2,1)S(1)}, u32[]{:S(2)}, u32[]{:S(2)}) collective-permute-start(bf16[256,512]{1,0:T(8,128)(2,1)S(1)} %slice.108), channel_id=1, source_target_pairs={{0,18},{1,19},{2,16},{3,17},{4,22},{5,23},{6,20},{7,21},{8,26},{9,... | collective-permute-start | bytes 786440 | tf_op jit(solution)/shard_map/ppermute | solution.py:26
  156.6 16.4 %collective-permute-start.24 = (bf16[256,512]{1,0:T(8,128)(2,1)S(1)}, bf16[256,512]{1,0:T(8,128)(2,1)S(1)}, u32[]{:S(2)}, u32[]{:S(2)}) collective-permute-start(bf16[256,512]{1,0:T(8,128)(2,1)S(1)} %fusion.54), channel_id=1, source_target_pairs={{0,16},{1,17},{2,18},{3,19},{4,20},{5,21},{6,22},{7,23},{8,24},{9,... | collective-permute-start | bytes 786440 | tf_op jit(solution)/shard_map/ppermute | solution.py:26
  158.5 22.1 %collective-permute-start.29 = (bf16[256,512]{1,0:T(8,128)(2,1)S(1)}, bf16[256,512]{1,0:T(8,128)(2,1)S(1)}, u32[]{:S(2)}, u32[]{:S(2)}) collective-permute-start(bf16[256,512]{1,0:T(8,128)(2,1)S(1)} %fusion.55), channel_id=1, source_target_pairs={{0,16},{1,17},{2,18},{3,19},{4,20},{5,21},{6,22},{7,23},{8,24},{9,... | collective-permute-start | bytes 786440 | tf_op jit(solution)/shard_map/ppermute | solution.py:26
  164.1 22.8 %collective-permute-start.36 = (bf16[256,512]{1,0:T(8,128)(2,1)S(1)}, bf16[256,512]{1,0:T(8,128)(2,1)S(1)}, u32[]{:S(2)}, u32[]{:S(2)}) collective-permute-start(bf16[256,512]{1,0:T(8,128)(2,1)S(1)} %fusion.56), channel_id=1, source_target_pairs={{0,16},{1,17},{2,18},{3,19},{4,20},{5,21},{6,22},{7,23},{8,24},{9,... | collective-permute-start | bytes 786440 | tf_op jit(solution)/shard_map/ppermute | solution.py:26
  173.7 11.9 %collective-permute-start.18 = (bf16[256,512]{1,0:T(8,128)(2,1)S(1)}, bf16[256,512]{1,0:T(8,128)(2,1)S(1)}, u32[]{:S(2)}, u32[]{:S(2)}) collective-permute-start(bf16[256,512]{1,0:T(8,128)(2,1)S(1)} %get-tuple-element.29), channel_id=1, source_target_pairs={{0,32},{1,97},{2,34},{3,99},{4,36},{5,101},{6,38},{7,103},{8,40},{... | collective-permute-start | bytes 786440 | tf_op jit(solution)/shard_map/ppermute | solution.py:26
  180.8 8.6 %collective-permute-start.17 = (bf16[256,512]{1,0:T(8,128)(2,1)S(1)}, bf16[256,512]{1,0:T(8,128)(2,1)S(1)}, u32[]{:S(2)}, u32[]{:S(2)}) collective-permute-start(bf16[256,512]{1,0:T(8,128)(2,1)S(1)} %get-tuple-element.28), channel_id=1, source_target_pairs={{0,32},{1,97},{2,34},{3,99},{4,36},{5,101},{6,38},{7,103},{8,40},{... | collective-permute-start | bytes 786440 | tf_op jit(solution)/shard_map/ppermute | solution.py:26
  185.7 6.3 %collective-permute-start.19 = (bf16[256,512]{1,0:T(8,128)(2,1)S(1)}, bf16[256,512]{1,0:T(8,128)(2,1)S(1)}, u32[]{:S(2)}, u32[]{:S(2)}) collective-permute-start(bf16[256,512]{1,0:T(8,128)(2,1)S(1)} %fusion.52), channel_id=1, source_target_pairs={{0,96},{1,33},{2,98},{3,35},{4,100},{5,37},{6,102},{7,39},{8,104},... | collective-permute-start | bytes 786440 | tf_op jit(solution)/shard_map/ppermute | solution.py:26

commit v3 on v2

v3 whole, which is shorter than its diff:
```python
import itertools

import jax
import jax.numpy as jnp
from jax import lax
from jax.sharding import Mesh
from jax.sharding import PartitionSpec as P

AXES = ("z", "l", "x", "h", "c")
SAMP = ("z", "l")
FEAT = ("x", "h", "c")
SIZES = (4, 2, 4, 2, 2)
F32 = jnp.float32
BF16 = jnp.bfloat16


def send(value, route):
    pairs = []
    for source, at in enumerate(itertools.product(*map(range, SIZES))):
        target = route(*at)
        if target is not None:
            index = 0
            for size, place in zip(SIZES, target):
                index = index * size + place % size
            pairs.append((source, index))
    return lax.ppermute(value, AXES, pairs)


def core_swap(value):
    return send(value, lambda z, l, x, h, c: (z, l, x, h, 1 - c))


def with_y(z, l, x, h, c):
    y = 2 * h + l + 1 - 2 * c
    return (z, y % 2, x, y // 2 % 2, c)


def against_y(z, l, x, h, c):
    y = 2 * h + l - 1 + 2 * c
    return (z, y % 2, x, y // 2 % 2, c)


def near_route(z, l, x, h, c):
    return (z ^ 1 if c == 0 else 3 - z, l, x, h, c)


def over_route(z, l, x, h, c):
    return (3 - z if c == 0 else z ^ 1, l, x, h, c)


def with_ring(z, l, x, h, c):
    return (z, l, x + 1 - 2 * c, h, c)


def against_ring(z, l, x, h, c):
    return (z, l, x - 1 + 2 * c, h, c)


def sum_over_l(same, other, keeps, tail=None):
    there = send(other.astype(BF16), lambda z, l, x, h, c: (z, 1 - l, x, 1 - h, c))
    back = jnp.where(keeps, there, same.astype(BF16))
    if tail is not None:
        back = with_tail(back, tail)
    back = send(back, lambda z, l, x, h, c: (z, 1 - l, x, h, c))
    return same, there, back


def joined_sum(keeps, same, there, back):
    return jnp.where(keeps, same.astype(F32), there.astype(F32)) + back.astype(F32)


def with_tail(block, tail):
    high = lax.reduce_precision(tail, 8, 7)
    row = jnp.concatenate([high, tail - high]).astype(BF16).reshape(-1, block.shape[1])
    return jnp.concatenate([block, jnp.pad(row, ((0, 16 - row.shape[0]), (0, 0)))], axis=0)


def split_tail(block, length):
    row = block[-16:].reshape(-1)[: 2 * length].astype(F32)
    return block[:-16], row[:length] + row[length:]


def product(rows, weighted):
    return lax.dot_general(
        rows, weighted, (((0,), (0,)), ((), ())), preferred_element_type=F32
    ).astype(BF16)


def per_device(design, labels, coef_all, active, penalty):
    z, l, x, h, c = (lax.axis_index(name) for name in AXES)
    keeps = l == h
    scale = 1.0 / jnp.sqrt(F32(design.shape[0] * 8))
    half = design.shape[1] // 2

    def halves(array):
        return array[:, :half], array[:, half:]

    first = send(design, with_ring)
    beside = send(send(design, with_y), with_y)
    across = core_swap(design)
    beta = coef_all[active]
    part = jnp.dot(design, beta.astype(BF16), preferred_element_type=F32)
    part = part + send(send(part, against_y), against_y)
    one = send(part, against_ring)
    two = send(one, against_ring)
    part = part + one + two + send(two, against_ring)
    mine = [None, None]
    second = [None, None]
    far = [None, None]
    mine[0], _ = lax.optimization_barrier((design[:, :half], one))
    second[0] = send(mine[0], against_ring)
    far[0] = send(lax.optimization_barrier(first[:, :half]), with_ring)
    mine[1] = lax.optimization_barrier((design, part))[0][:, half:]
    second[1] = send(mine[1], against_ring)
    first_late = lax.optimization_barrier((first, part))[0][:, half:]
    far[1] = send(first_late, with_ring)
    margin = part + core_swap(part)
    prob = 1.0 / (1.0 + jnp.exp(-margin))
    weight = prob * (1.0 - prob)
    resid_b = (prob - labels.astype(F32)).astype(BF16)
    grad = jnp.dot(resid_b, design, preferred_element_type=F32)

    def weigh(block):
        return (block.astype(F32) * weight[:, None]).astype(BF16)

    places = {
        "q": z ^ 2,
        "p": jnp.where(c == 0, z ^ 1, 3 - z),
        "s": jnp.where(c == 0, 3 - z, z ^ 1),
        "z": z,
    }

    def pick(*block):
        return lax.optimization_barrier(jnp.stack(block))

    first_across = core_swap(first)

    def rows_of(k):
        own = pick(mine[k], second[k], far[k], halves(first)[k])
        other = pick(
            halves(across)[k], halves(first_across)[k], core_swap(far[k]), core_swap(second[k])
        )
        return own, other

    rows_y, rows_p = rows_of(0)
    beside, rows_y = lax.optimization_barrier((beside, rows_y))
    both = jnp.concatenate([weigh(design), weigh(beside)], axis=1)
    both = lax.optimization_barrier(both)

    def products(rows):
        def at(name):
            j = ((places[name] - x) * (1 - 2 * c)) % 4
            return product(lax.dynamic_index_in_dim(rows, j, 0, keepdims=False), both)

        return {name: at(name) for name in "qpsz"}

    def sum_over_z(terms, tail=None):
        near_side = send(terms["p"].astype(BF16), near_route)
        far_side = send(terms["q"], near_route)
        if tail is not None:
            far_side, more = split_tail(far_side, tail.shape[0])
            tail = tail + more
        passed = (terms["s"].astype(F32) + far_side.astype(F32)).astype(BF16)
        if tail is not None:
            passed = with_tail(passed, tail)
        over_side = send(passed, over_route)
        if tail is not None:
            over_side, more = split_tail(over_side, tail.shape[0])
            tail = tail + more
        return terms["z"].astype(F32) + near_side.astype(F32) + over_side.astype(F32), tail

    width = design.shape[1]
    terms = products(rows_y)
    joined = jnp.concatenate(list(terms.values()), axis=0)
    rows_p, _ = lax.optimization_barrier((rows_p, joined))
    summed = joined_sum(keeps, *sum_over_l(joined[:, :width], joined[:, width:], keeps))
    terms = dict(zip(terms, jnp.split(summed, 4)))
    terms["q"] = terms["q"].astype(BF16)
    block_y, _ = sum_over_z(terms)
    terms = products(rows_p)
    terms["q"] = with_tail(terms["q"], grad)
    far[1], second[1], _, _ = lax.optimization_barrier(
        (far[1], second[1], terms["q"], terms["p"])
    )
    total, grad = sum_over_z(terms, grad)
    sums_p = sum_over_l(total[:, :width], total[:, width:], keeps, grad)
    rows_o, rows_q = rows_of(1)
    total, _ = sum_over_z(products(rows_o))
    sums_o = sum_over_l(total[:, :width], total[:, width:], keeps)
    total, _ = sum_over_z(products(rows_q))
    sums_q = sum_over_l(total[:, :width], total[:, width:], keeps)
    back_p, back_o, _ = lax.optimization_barrier((sums_p[2], sums_o[2], sums_q[2]))
    back_p, more = split_tail(back_p, grad.shape[0])
    gradient = (grad + more) * scale + penalty * beta
    blocks = [
        block_y,
        joined_sum(keeps, *sums_p[:2], back_p),
        joined_sum(keeps, *sums_o[:2], back_o),
        joined_sum(keeps, *sums_q),
    ]
    ours = jnp.concatenate([blocks[0], blocks[2]], axis=0) * scale
    theirs = jnp.concatenate([blocks[1], blocks[3]], axis=0) * scale
    top = jnp.where(c == 0, ours, theirs)
    low = jnp.where(c == 0, theirs, ours)
    return (jnp.concatenate([top, low], axis=0), gradient)


def solution(mesh):
    split = Mesh(mesh.devices.reshape(SIZES), AXES)
    placed = (P(SAMP, FEAT), P(SAMP), P(), P(FEAT), P(FEAT))

    return jax.shard_map(
        per_device, mesh=split, in_specs=placed, out_specs=(P(SAMP, FEAT), P(FEAT)), check_vma=False
    )
```

time: 194 us -> 172 us (0.89)
  starting transfers between devices: 77.1 us -> 47.2 us
  other arithmetic: 9.87 us -> 15.2 us
  matrix products: 18.4 us -> 22.4 us
    ppermute x40 -> x39, starting transfers between devices: 77.1 us -> 47.2 us  [send(): return lax.ppermute(value, AXES, pairs)]
    dot_general x16, matrix products: 16.1 us -> 20.1 us  [product(): lax.dot_general(rows, weighted, (((0,), (0,)), ((), ())), preferred_eleme...]
    another operation x3 -> x4, local copies, waits for them, and re-layouts: 5.73 us -> 1.83 us  [pick(): return lax.optimization_barrier(jnp.stack(block))]
    select_n x4, other arithmetic: 0.24 us -> 3.44 us  [sum_over_l(): back = jnp.where(keeps, there, same.astype(BF16))]
    another operation x4, other arithmetic: 4.24 us -> 1.7 us  [pick(): return lax.optimization_barrier(jnp.stack(block))]
    slice x5 -> x6, local copies, waits for them, and re-layouts: 1.44 us -> 3.74 us  [the longest x1 1.79 us: per_device(): sums_o = sum_over_l(total[:, :width], total[:, width:], keeps)]
    add x7 -> x8, other arithmetic: 0.9 us -> 2.92 us  [the longest x3 2.31 us: joined_sum(): jnp.where(keeps, same.astype(F32), there.astype(F32)) + back.astype(F32)]
    ppermute x40 -> x39, waiting for transfers between devices: 73.7 us -> 73 us  [send(): return lax.ppermute(value, AXES, pairs)]
  transfers between devices with their start and end apart: 40 -> 39, of which waited for: 21 -> 18; matrix products, arithmetic and copies ran while one was open for 21% -> 28% of each run, Pallas kernels for 0% -> 0%
where the time goes in v3:
time: 172 us; the launch traced here: 171 us
  waiting for transfers between devices  73 us (42%)
  starting transfers between devices  47.2 us (27%)
  matrix products  22.4 us (13%)
  other arithmetic  15.2 us (9%)
  local copies, waits for them, and re-layouts  12.2 us (7%)
    ppermute x39, waiting for transfers between devices, send(): return lax.ppermute(value, AXES, pairs)  73 us
    ppermute x39, starting transfers between devices, send(): return lax.ppermute(value, AXES, pairs)  47.2 us
    dot_general x16, matrix products, product(): lax.dot_general(rows, weighted, (((0,), (0,)), ((), ())), preferred_eleme...  20.1 us
    gather x1, local copies, waits for them, and re-layouts, per_device(): beta = coef_all[active]  6.5 us
  transfers between devices with their start and end apart: 39, of which 18 were waited for; matrix products, arithmetic and copies ran while one was open for 28% of the time, Pallas kernels for 0%

profile of v3, /device:TPU:1, one launch (start us, length us, event | category | flops | bytes accessed | tf_op | source)
XLA Modules:
  0.0 171.2 jit_solution(2773730101494181112)
XLA Ops:
  0.6 3.4 %collective-permute-start.6 = (bf16[1536,512]{1,0:T(8,128)(2,1)}, bf16[1536,512]{1,0:T(8,128)(2,1)S(1)}, u32[]{:S(2)}, u32[]{:S(2)}) collective-permute-start(bf16[1536,512]{1,0:T(8,128)(2,1)} %param.5), channel_id=1, source_target_pairs={{0,4},{1,13},{2,6},{3,15},{4,8},{5,1},{6,10},{7,3},{8,12},{9,5},{1... | collective-permute-start | bytes 4718600 | tf_op jit(solution)/shard_map/ppermute | solution.py:26
  4.0 2.7 %collective-permute-start = (bf16[1536,512]{1,0:T(8,128)(2,1)}, bf16[1536,512]{1,0:T(8,128)(2,1)}, u32[]{:S(2)}, u32[]{:S(2)}) collective-permute-start(bf16[1536,512]{1,0:T(8,128)(2,1)} %param.5), channel_id=1, source_target_pairs={{0,16},{1,19},{2,18},{3,17},{4,20},{5,23},{6,22},{7,21},{8,24},{9,... | collective-permute-start | bytes 4718600 | tf_op jit(solution)/shard_map/ppermute | solution.py:26
  7.4 6.5 %gather_fusion = f32[512]{0:T(512)S(1)} fusion(f32[1048576]{0:T(1024)} %param.7, s32[1024]{0:T(1024)S(1)} %pad_clamp_fusion), kind=kCustom, calls=%fused_computation | custom fusion | bytes 6144 | tf_op jit(solution)/shard_map/gather | solution.py:101
  14.0 1.9 %convolution_reduce_fusion = f32[1536]{0:T(1024)S(1)} fusion(bf16[512,1]{0,1:T(2,128)(2,1)S(1)} %reshape.99, bf16[1536,512]{1,0:T(8,128)(2,1)} %param.5), kind=kOutput, calls=%fused_computation.33 | convolution fusion | flops 1572864 | bytes 1580032 | tf_op jit(solution)/shard_map/dot_general | solution.py:102
  16.0 4.2 %collective-permute-done.2 = f32[1536]{0:T(1024)S(1)} collective-permute-done((f32[1536]{0:T(1024)S(1)}, f32[1536]{0:T(1024)S(1)}, u32[]{:S(2)}, u32[]{:S(2)}) %collective-permute-start.2) | collective-permute-done | bytes 6176 | tf_op jit(solution)/shard_map/ppermute | solution.py:26
  20.2 4.2 %collective-permute-done.3 = f32[1536]{0:T(1024)S(1)} collective-permute-done((f32[1536]{0:T(1024)S(1)}, f32[1536]{0:T(1024)S(1)}, u32[]{:S(2)}, u32[]{:S(2)}) %collective-permute-start.3) | collective-permute-done | bytes 6176 | tf_op jit(solution)/shard_map/ppermute | solution.py:26
  24.4 3.7 %collective-permute-done.4 = f32[1536]{0:T(1024)S(1)} collective-permute-done((f32[1536]{0:T(1024)S(1)}, f32[1536]{0:T(1024)S(1)}, u32[]{:S(2)}, u32[]{:S(2)}) %collective-permute-start.4) | collective-permute-done | bytes 6176 | tf_op jit(solution)/shard_map/ppermute | solution.py:26
  28.1 3.7 %collective-permute-done.8 = f32[1536]{0:T(1024)S(1)} collective-permute-done((f32[1536]{0:T(1024)S(1)}, f32[1536]{0:T(1024)S(1)}, u32[]{:S(2)}, u32[]{:S(2)}) %collective-permute-start.8) | collective-permute-done | bytes 6176 | tf_op jit(solution)/shard_map/ppermute | solution.py:26
  31.8 2.0 %collective-permute-start.18 = (bf16[1536,512]{1,0:T(8,128)(2,1)S(1)}, bf16[1536,512]{1,0:T(8,128)(2,1)}, u32[]{:S(2)}, u32[]{:S(2)}) collective-permute-start(bf16[1536,512]{1,0:T(8,128)(2,1)S(1)} %copy-done), channel_id=1, source_target_pairs={{0,1},{1,0},{2,3},{3,2},{4,5},{5,4},{6,7},{7,6},{8,9},{9,8},{10,11... | collective-permute-start | bytes 4718600 | tf_op jit(solution)/shard_map/ppermute | solution.py:26
  37.8 3.2 %collective-permute-start.1 = (bf16[1536,512]{1,0:T(8,128)(2,1)}, bf16[1536,512]{1,0:T(8,128)(2,1)S(1)}, u32[]{:S(2)}, u32[]{:S(2)}) collective-permute-start(bf16[1536,512]{1,0:T(8,128)(2,1)} %collective-permute-done), channel_id=1, source_target_pairs={{0,16},{1,19},{2,18},{3,17},{4,20},{5,23},{6,22},{7,21},{8,24},{9,... | collective-permute-start | bytes 4718600 | tf_op jit(solution)/shard_map/ppermute | solution.py:26
  41.2 2.3 %collective-permute-start.7 = (bf16[1536,256]{1,0:T(8,128)(2,1)S(1)}, bf16[1536,256]{1,0:T(8,128)(2,1)S(1)}, u32[]{:S(2)}, u32[]{:S(2)}) collective-permute-start(bf16[1536,256]{1,0:T(8,128)(2,1)S(1)} %get-tuple-element.34), channel_id=1, source_target_pairs={{0,4},{1,13},{2,6},{3,15},{4,8},{5,1},{6,10},{7,3},{8,12},{9,5},{1... | collective-permute-start | bytes 2359304 | tf_op jit(solution)/shard_map/ppermute | solution.py:26
  43.6 7.4 %collective-permute-done.5 = bf16[1536,256]{1,0:T(8,128)(2,1)S(1)} collective-permute-done((bf16[1536,256]{1,0:T(8,128)(2,1)}, bf16[1536,256]{1,0:T(8,128)(2,1)S(1)}, u32[]{:S(2)}, u32[]{:S(2)}) %collective-permute-start.5) | collective-permute-done | bytes 786464 | tf_op jit(solution)/shard_map/ppermute | solution.py:26
  51.1 1.5 slice_bitcast_fusion.1
  52.6 4.7 %collective-permute-done.7 = bf16[1536,256]{1,0:T(8,128)(2,1)S(1)} collective-permute-done((bf16[1536,256]{1,0:T(8,128)(2,1)S(1)}, bf16[1536,256]{1,0:T(8,128)(2,1)S(1)}, u32[]{:S(2)}, u32[]{:S(2)}) %collective-permute-start.7) | collective-permute-done | bytes 786464 | tf_op jit(solution)/shard_map/ppermute | solution.py:26
  58.7 2.2 %collective-permute-start.16 = (bf16[1536,256]{1,0:T(8,128)(2,1)S(1)}, bf16[1536,256]{1,0:T(8,128)(2,1)S(1)}, u32[]{:S(2)}, u32[]{:S(2)}) collective-permute-start(bf16[1536,256]{1,0:T(8,128)(2,1)S(1)} %slice.111), channel_id=1, source_target_pairs={{0,4},{1,13},{2,6},{3,15},{4,8},{5,1},{6,10},{7,3},{8,12},{9,5},{1... | collective-permute-start | bytes 2359304 | tf_op jit(solution)/shard_map/ppermute | solution.py:26
  67.0 1.0 convolution_convert_fusion.10
  68.0 3.9 %collective-permute-start.26 = (bf16[256,1024]{1,0:T(8,128)(2,1)S(1)}, bf16[256,1024]{1,0:T(8,128)(2,1)S(1)}, u32[]{:S(2)}, u32[]{:S(2)}) collective-permute-start(bf16[256,1024]{1,0:T(8,128)(2,1)S(1)} %convolution_convert_fusion.10), channel_id=1, source_target_pairs={{0,32},{1,97},{2,34},{3,99},{4,36},{5,101},{6,38},{7,103},{8,40},{... | collective-permute-start | bytes 1572872 | tf_op jit(solution)/shard_map/ppermute | solution.py:26
  75.2 3.5 %collective-permute-start.23 = (bf16[256,1024]{1,0:T(8,128)(2,1)S(1)}, bf16[256,1024]{1,0:T(8,128)(2,1)S(1)}, u32[]{:S(2)}, u32[]{:S(2)}) collective-permute-start(bf16[256,1024]{1,0:T(8,128)(2,1)S(1)} %convolution_convert_fusion.6), channel_id=1, source_target_pairs={{0,32},{1,97},{2,34},{3,99},{4,36},{5,101},{6,38},{7,103},{8,40},{... | collective-permute-start | bytes 1572872 | tf_op jit(solution)/shard_map/ppermute | solution.py:26
  80.7 9.4 %collective-permute-done.23 = bf16[256,1024]{1,0:T(8,128)(2,1)S(1)} collective-permute-done((bf16[256,1024]{1,0:T(8,128)(2,1)S(1)}, bf16[256,1024]{1,0:T(8,128)(2,1)S(1)}, u32[]{:S(2)}, u32[]{:S(2)}) %collective-permute-start.23) | collective-permute-done | bytes 524320 | tf_op jit(solution)/shard_map/ppermute | solution.py:26
  90.1 3.3 %collective-permute-start.11 = (bf16[1024,512]{1,0:T(8,128)(2,1)S(1)}, bf16[1024,512]{1,0:T(8,128)(2,1)S(1)}, u32[]{:S(2)}, u32[]{:S(2)}) collective-permute-start(bf16[1024,512]{1,0:T(8,128)(2,1)S(1)} %slice.139), channel_id=1, source_target_pairs={{0,18},{1,19},{2,16},{3,17},{4,22},{5,23},{6,20},{7,21},{8,26},{9,... | collective-permute-start | bytes 3145736 | tf_op jit(solution)/shard_map/ppermute | solution.py:26
  93.4 1.0 add_convert_fusion.2
  94.5 2.7 %collective-permute-start.22 = (bf16[256,1024]{1,0:T(8,128)(2,1)S(1)}, bf16[256,1024]{1,0:T(8,128)(2,1)S(1)}, u32[]{:S(2)}, u32[]{:S(2)}) collective-permute-start(bf16[256,1024]{1,0:T(8,128)(2,1)S(1)} %convolution_convert_fusion.8), channel_id=1, source_target_pairs={{0,32},{1,97},{2,34},{3,99},{4,36},{5,101},{6,38},{7,103},{8,40},{... | collective-permute-start | bytes 1572872 | tf_op jit(solution)/shard_map/ppermute | solution.py:26
  97.3 1.0 add_convert_fusion.1
  98.7 1.4 collective-permute-start.28
  101.6 1.8 %convolution_convert_fusion.2 = bf16[256,1024]{1,0:T(8,128)(2,1)} fusion(bf16[1536,1024]{1,0:T(8,128)(2,1)S(1)} %pad_maximum_fusion.1, bf16[4,1536,256]{2,1,0:T(8,128)(2,1)S(1)} %pad_maximum_fusion.4, s32[]{:T(128)S(6)} %select_n.140), kind=kOutput, calls=%fused_computation.14 | convolution fusion | flops 805568512 | bytes 4456452 | tf_op jit(solution)/shard_map/dot_general | solution.py:84
  103.4 12.2 %collective-permute-done.11 = bf16[1024,512]{1,0:T(8,128)(2,1)S(1)} collective-permute-done((bf16[1024,512]{1,0:T(8,128)(2,1)S(1)}, bf16[1024,512]{1,0:T(8,128)(2,1)S(1)}, u32[]{:S(2)}, u32[]{:S(2)}) %collective-permute-start.11) | collective-permute-done | bytes 1048608 | tf_op jit(solution)/shard_map/ppermute | solution.py:26
  115.6 3.6 %collective-permute-start.34 = (bf16[256,1024]{1,0:T(8,128)(2,1)}, bf16[256,1024]{1,0:T(8,128)(2,1)}, u32[]{:S(2)}, u32[]{:S(2)}) collective-permute-start(bf16[256,1024]{1,0:T(8,128)(2,1)} %convolution_convert_fusion.2), channel_id=1, source_target_pairs={{0,32},{1,97},{2,34},{3,99},{4,36},{5,101},{6,38},{7,103},{8,40},{... | collective-permute-start | bytes 1572872 | tf_op jit(solution)/shard_map/ppermute | solution.py:26
  119.1 1.2 broadcast_select_fusion
  120.4 1.2 convert_add_fusion.3
  121.6 1.8 %slice.199 = bf16[256,512]{1,0:T(8,128)(2,1)} slice(f32[256,1024]{1,0:T(8,128)} %convert_add_fusion.3), slice={[0:256], [512:1024]} | slice | bytes 524288 | tf_op jit(solution)/shard_map/slice | solution.py:189
  123.4 1.7 %collective-permute-start.25 = (bf16[256,512]{1,0:T(8,128)(2,1)}, bf16[256,512]{1,0:T(8,128)(2,1)S(1)}, u32[]{:S(2)}, u32[]{:S(2)}) collective-permute-start(bf16[256,512]{1,0:T(8,128)(2,1)} %slice.199), channel_id=1, source_target_pairs={{0,18},{1,19},{2,16},{3,17},{4,22},{5,23},{6,20},{7,21},{8,26},{9,... | collective-permute-start | bytes 786440 | tf_op jit(solution)/shard_map/ppermute | solution.py:26
  128.0 4.0 %collective-permute-done.35 = bf16[256,1024]{1,0:T(8,128)(2,1)S(1)} collective-permute-done((bf16[256,1024]{1,0:T(8,128)(2,1)S(1)}, bf16[256,1024]{1,0:T(8,128)(2,1)S(1)}, u32[]{:S(2)}, u32[]{:S(2)}) %collective-permute-start.35) | collective-permute-done | bytes 524320 | tf_op jit(solution)/shard_map/ppermute | solution.py:26
  131.9 1.8 %add_convert_fusion = bf16[256,1024]{1,0:T(8,128)(2,1)} fusion(bf16[256,1024]{1,0:T(8,128)(2,1)S(1)} %collective-permute-done.35, bf16[1536,1024]{1,0:T(8,128)(2,1)S(1)} %pad_maximum_fusion.1, bf16[4,1536,256]{2,1,0:T(8,128)(2,1)S(1)} %pad_maximum_fusion.4, s32[]{:T(128)S(6)} %select_n.143), kind=kOutput, calls=%fused_computation.37 | convolution fusion | flops 806617088 | bytes 4980740 | tf_op jit(solution)/shard_map/dot_general | solution.py:84
  133.8 1.1 fusion.50
  135.0 2.3 %collective-permute-done.29 = bf16[256,512]{1,0:T(8,128)(2,1)} collective-permute-done((bf16[256,512]{1,0:T(8,128)(2,1)}, bf16[256,512]{1,0:T(8,128)(2,1)}, u32[]{:S(2)}, u32[]{:S(2)}) %collective-permute-start.29) | collective-permute-done | bytes 262176 | tf_op jit(solution)/shard_map/ppermute | solution.py:26
  137.2 1.2 fusion.51
  138.4 4.0 %collective-permute-done.36 = bf16[256,1024]{1,0:T(8,128)(2,1)} collective-permute-done((bf16[256,1024]{1,0:T(8,128)(2,1)}, bf16[256,1024]{1,0:T(8,128)(2,1)}, u32[]{:S(2)}, u32[]{:S(2)}) %collective-permute-start.36) | collective-permute-done | bytes 524320 | tf_op jit(solution)/shard_map/ppermute | solution.py:26
  142.4 3.4 %convert_add_fusion.1 = f32[256,1024]{1,0:T(8,128)S(1)} fusion(bf16[256,1024]{1,0:T(8,128)(2,1)} %collective-permute-done.36, bf16[256,1024]{1,0:T(8,128)(2,1)} %collective-permute-done.34, bf16[1536,1024]{1,0:T(8,128)(2,1)} %copy-done.2, bf16[4,1536,256]{2,1,0:T(8,128)(2,1)} %copy-done.3, s32[]{:T(128)S(6)} %select_n.145), kind=kOutput, calls=%fused_computation.36 | convolution fusion | flops 806879232 | bytes 6029316 | tf_op jit(solution)/shard_map/dot_general | solution.py:84
  145.8 1.8 %collective-permute-start.37 = (bf16[256,512]{1,0:T(8,128)(2,1)S(1)}, bf16[256,512]{1,0:T(8,128)(2,1)S(1)}, u32[]{:S(2)}, u32[]{:S(2)}) collective-permute-start(bf16[256,512]{1,0:T(8,128)(2,1)S(1)} %slice.197), channel_id=1, source_target_pairs={{0,18},{1,19},{2,16},{3,17},{4,22},{5,23},{6,20},{7,21},{8,26},{9,... | collective-permute-start | bytes 786440 | tf_op jit(solution)/shard_map/ppermute | solution.py:26
  147.6 1.8 %fusion.82 = (bf16[1024,512]{1,0:T(8,128)(2,1)S(1)}, f32[1024,512]{1,0:T(8,128)S(1)}) fusion(bf16[1024,512]{1,0:T(8,128)(2,1)} %collective-permute-done.12, bf16[1024,512]{1,0:T(8,128)(2,1)S(1)} %collective-permute-done.11, bf16[1024,1024]{1,0:T(8,128)(2,1)S(1)} %pad_maximum_fusion.5, pred[]{:T(512)S(6)} %eq.27), kind=kLoop, calls=%fused_computation.151 | loop fusion | flops 3145728 | bytes 6291457 | tf_op jit(solution)/shard_map/convert.14
  149.5 2.6 %collective-permute-start.14 = (bf16[256,512]{1,0:T(8,128)(2,1)S(1)}, bf16[256,512]{1,0:T(8,128)(2,1)S(1)}, u32[]{:S(2)}, u32[]{:S(2)}) collective-permute-start(bf16[256,512]{1,0:T(8,128)(2,1)S(1)} %get-tuple-element.40), channel_id=1, source_target_pairs={{0,32},{1,97},{2,34},{3,99},{4,36},{5,101},{6,38},{7,103},{8,40},{... | collective-permute-start | bytes 786440 | tf_op jit(solution)/shard_map/ppermute | solution.py:26
  152.3 1.1 collective-permute-done.37
  153.9 1.9 %collective-permute-start.13 = (bf16[256,512]{1,0:T(8,128)(2,1)S(1)}, bf16[256,512]{1,0:T(8,128)(2,1)S(1)}, u32[]{:S(2)}, u32[]{:S(2)}) collective-permute-start(bf16[256,512]{1,0:T(8,128)(2,1)S(1)} %get-tuple-element.39), channel_id=1, source_target_pairs={{0,32},{1,97},{2,34},{3,99},{4,36},{5,101},{6,38},{7,103},{8,40},{... | collective-permute-start | bytes 786440 | tf_op jit(solution)/shard_map/ppermute | solution.py:26
  156.8 4.1 %collective-permute-done.30 = bf16[272,512]{1,0:T(8,128)(2,1)S(1)} collective-permute-done((bf16[272,512]{1,0:T(8,128)(2,1)S(1)}, bf16[272,512]{1,0:T(8,128)(2,1)S(1)}, u32[]{:S(2)}, u32[]{:S(2)}) %collective-permute-start.30) | collective-permute-done | bytes 278560 | tf_op jit(solution)/shard_map/ppermute | solution.py:26
  160.9 5.3 %collective-permute-done.38 = bf16[256,512]{1,0:T(8,128)(2,1)S(1)} collective-permute-done((bf16[256,512]{1,0:T(8,128)(2,1)S(1)}, bf16[256,512]{1,0:T(8,128)(2,1)S(1)}, u32[]{:S(2)}, u32[]{:S(2)}) %collective-permute-start.38) | collective-permute-done | bytes 262176 | tf_op jit(solution)/shard_map/ppermute | solution.py:26
  167.0 1.1 convert_add_fusion.5
  168.0 1.2 convert_add_fusion.6
  169.7 1.5 pad_maximum_fusion.6
  (127 shorter events, 25.4 us)
Async XLA Ops:
  0.6 31.2 %copy-start = (bf16[1536,512]{1,0:T(8,128)(2,1)S(1)}, bf16[1536,512]{1,0:T(8,128)(2,1)}, u32[]{:S(2)}) copy-start(bf16[1536,512]{1,0:T(8,128)(2,1)} %param.5) | copy-start | bytes 4718596
  0.6 36.8 %collective-permute-start.6 = (bf16[1536,512]{1,0:T(8,128)(2,1)}, bf16[1536,512]{1,0:T(8,128)(2,1)S(1)}, u32[]{:S(2)}, u32[]{:S(2)}) collective-permute-start(bf16[1536,512]{1,0:T(8,128)(2,1)} %param.5), channel_id=1, source_target_pairs={{0,4},{1,13},{2,6},{3,15},{4,8},{5,1},{6,10},{7,3},{8,12},{9,5},{1... | collective-permute-start | bytes 4718600 | tf_op jit(solution)/shard_map/ppermute | solution.py:26
  4.0 33.8 %collective-permute-start = (bf16[1536,512]{1,0:T(8,128)(2,1)}, bf16[1536,512]{1,0:T(8,128)(2,1)}, u32[]{:S(2)}, u32[]{:S(2)}) collective-permute-start(bf16[1536,512]{1,0:T(8,128)(2,1)} %param.5), channel_id=1, source_target_pairs={{0,16},{1,19},{2,18},{3,17},{4,20},{5,23},{6,22},{7,21},{8,24},{9,... | collective-permute-start | bytes 4718600 | tf_op jit(solution)/shard_map/ppermute | solution.py:26
  13.9 23.2 %copy-start.6 = (s32[1536]{0:T(1024)S(1)}, s32[1536]{0:T(1024)}, u32[]{:S(2)}) copy-start(s32[1536]{0:T(1024)} %param.6) | copy-start | bytes 18436
  15.9 4.3 %collective-permute-start.2 = (f32[1536]{0:T(1024)S(1)}, f32[1536]{0:T(1024)S(1)}, u32[]{:S(2)}, u32[]{:S(2)}) collective-permute-start(f32[1536]{0:T(1024)S(1)} %convolution_reduce_fusion), channel_id=1, source_target_pairs={{0,18},{1,17},{2,16},{3,19},{4,22},{5,21},{6,20},{7,23},{8,26},{9,... | collective-permute-start | bytes 18440 | tf_op jit(solution)/shard_map/ppermute | solution.py:26
  20.2 4.2 %collective-permute-start.3 = (f32[1536]{0:T(1024)S(1)}, f32[1536]{0:T(1024)S(1)}, u32[]{:S(2)}, u32[]{:S(2)}) collective-permute-start(f32[1536]{0:T(1024)S(1)} %collective-permute-done.2), channel_id=1, source_target_pairs={{0,18},{1,17},{2,16},{3,19},{4,22},{5,21},{6,20},{7,23},{8,26},{9,... | collective-permute-start | bytes 18440 | tf_op jit(solution)/shard_map/ppermute | solution.py:26
  24.4 3.7 %collective-permute-start.4 = (f32[1536]{0:T(1024)S(1)}, f32[1536]{0:T(1024)S(1)}, u32[]{:S(2)}, u32[]{:S(2)}) collective-permute-start(f32[1536]{0:T(1024)S(1)} %add.160), channel_id=1, source_target_pairs={{0,12},{1,5},{2,14},{3,7},{4,0},{5,9},{6,2},{7,11},{8,4},{9,13},{1... | collective-permute-start | bytes 18440 | tf_op jit(solution)/shard_map/ppermute | solution.py:26
  28.1 3.7 %collective-permute-start.8 = (f32[1536]{0:T(1024)S(1)}, f32[1536]{0:T(1024)S(1)}, u32[]{:S(2)}, u32[]{:S(2)}) collective-permute-start(f32[1536]{0:T(1024)S(1)} %collective-permute-done.4), channel_id=1, source_target_pairs={{0,12},{1,5},{2,14},{3,7},{4,0},{5,9},{6,2},{7,11},{8,4},{9,13},{1... | collective-permute-start | bytes 18440 | tf_op jit(solution)/shard_map/ppermute | solution.py:26
  31.8 3.7 %collective-permute-start.9 = (f32[1536]{0:T(1024)S(1)}, f32[1536]{0:T(1024)S(1)}, u32[]{:S(2)}, u32[]{:S(2)}) collective-permute-start(f32[1536]{0:T(1024)S(1)} %collective-permute-done.8), channel_id=1, source_target_pairs={{0,12},{1,5},{2,14},{3,7},{4,0},{5,9},{6,2},{7,11},{8,4},{9,13},{1... | collective-permute-start | bytes 18440 | tf_op jit(solution)/shard_map/ppermute | solution.py:26
  31.8 19.2 %collective-permute-start.18 = (bf16[1536,512]{1,0:T(8,128)(2,1)S(1)}, bf16[1536,512]{1,0:T(8,128)(2,1)}, u32[]{:S(2)}, u32[]{:S(2)}) collective-permute-start(bf16[1536,512]{1,0:T(8,128)(2,1)S(1)} %copy-done), channel_id=1, source_target_pairs={{0,1},{1,0},{2,3},{3,2},{4,5},{5,4},{6,7},{7,6},{8,9},{9,8},{10,11... | collective-permute-start | bytes 4718600 | tf_op jit(solution)/shard_map/ppermute | solution.py:26
  34.8 16.2 %collective-permute-start.5 = (bf16[1536,256]{1,0:T(8,128)(2,1)}, bf16[1536,256]{1,0:T(8,128)(2,1)S(1)}, u32[]{:S(2)}, u32[]{:S(2)}) collective-permute-start(bf16[1536,256]{1,0:T(8,128)(2,1)} %slice.106), channel_id=1, source_target_pairs={{0,12},{1,5},{2,14},{3,7},{4,0},{5,9},{6,2},{7,11},{8,4},{9,13},{1... | collective-permute-start | bytes 2359304 | tf_op jit(solution)/shard_map/ppermute | solution.py:26
  35.5 1.6 collective-permute-start.10
  37.5 23.5 %collective-permute-start.19 = (bf16[1536,512]{1,0:T(8,128)(2,1)S(1)}, bf16[1536,512]{1,0:T(8,128)(2,1)S(1)}, u32[]{:S(2)}, u32[]{:S(2)}) collective-permute-start(bf16[1536,512]{1,0:T(8,128)(2,1)S(1)} %collective-permute-done.6), channel_id=1, source_target_pairs={{0,1},{1,0},{2,3},{3,2},{4,5},{5,4},{6,7},{7,6},{8,9},{9,8},{10,11... | collective-permute-start | bytes 4718600 | tf_op jit(solution)/shard_map/ppermute | solution.py:26
  37.8 20.9 %collective-permute-start.1 = (bf16[1536,512]{1,0:T(8,128)(2,1)}, bf16[1536,512]{1,0:T(8,128)(2,1)S(1)}, u32[]{:S(2)}, u32[]{:S(2)}) collective-permute-start(bf16[1536,512]{1,0:T(8,128)(2,1)} %collective-permute-done), channel_id=1, source_target_pairs={{0,16},{1,19},{2,18},{3,17},{4,20},{5,23},{6,22},{7,21},{8,24},{9,... | collective-permute-start | bytes 4718600 | tf_op jit(solution)/shard_map/ppermute | solution.py:26
  41.2 16.1 %copy-start.1 = (bf16[1536,256]{1,0:T(8,128)(2,1)S(1)}, bf16[1536,256]{1,0:T(8,128)(2,1)}, u32[]{:S(2)}) copy-start(bf16[1536,256]{1,0:T(8,128)(2,1)} %slice.106) | copy-start | bytes 2359300
  41.2 16.1 %collective-permute-start.7 = (bf16[1536,256]{1,0:T(8,128)(2,1)S(1)}, bf16[1536,256]{1,0:T(8,128)(2,1)S(1)}, u32[]{:S(2)}, u32[]{:S(2)}) collective-permute-start(bf16[1536,256]{1,0:T(8,128)(2,1)S(1)} %get-tuple-element.34), channel_id=1, source_target_pairs={{0,4},{1,13},{2,6},{3,15},{4,8},{5,1},{6,10},{7,3},{8,12},{9,5},{1... | collective-permute-start | bytes 2359304 | tf_op jit(solution)/shard_map/ppermute | solution.py:26
  51.0 22.1 %collective-permute-start.17 = (bf16[1536,256]{1,0:T(8,128)(2,1)S(1)}, bf16[1536,256]{1,0:T(8,128)(2,1)S(1)}, u32[]{:S(2)}, u32[]{:S(2)}) collective-permute-start(bf16[1536,256]{1,0:T(8,128)(2,1)S(1)} %get-tuple-element.31), channel_id=1, source_target_pairs={{0,12},{1,5},{2,14},{3,7},{4,0},{5,9},{6,2},{7,11},{8,4},{9,13},{1... | collective-permute-start | bytes 2359304 | tf_op jit(solution)/shard_map/ppermute | solution.py:26
  51.0 10.1 %collective-permute-start.21 = (bf16[1536,256]{1,0:T(8,128)(2,1)S(1)}, bf16[1536,256]{1,0:T(8,128)(2,1)S(1)}, u32[]{:S(2)}, u32[]{:S(2)}) collective-permute-start(bf16[1536,256]{1,0:T(8,128)(2,1)S(1)} %collective-permute-done.5), channel_id=1, source_target_pairs={{0,1},{1,0},{2,3},{3,2},{4,5},{5,4},{6,7},{7,6},{8,9},{9,8},{10,11... | collective-permute-start | bytes 2359304 | tf_op jit(solution)/shard_map/ppermute | solution.py:26
  57.3 3.8 %collective-permute-start.20 = (bf16[1536,256]{1,0:T(8,128)(2,1)S(1)}, bf16[1536,256]{1,0:T(8,128)(2,1)S(1)}, u32[]{:S(2)}, u32[]{:S(2)}) collective-permute-start(bf16[1536,256]{1,0:T(8,128)(2,1)S(1)} %collective-permute-done.7), channel_id=1, source_target_pairs={{0,1},{1,0},{2,3},{3,2},{4,5},{5,4},{6,7},{7,6},{8,9},{9,8},{10,11... | collective-permute-start | bytes 2359304 | tf_op jit(solution)/shard_map/ppermute | solution.py:26
  58.7 14.4 %collective-permute-start.16 = (bf16[1536,256]{1,0:T(8,128)(2,1)S(1)}, bf16[1536,256]{1,0:T(8,128)(2,1)S(1)}, u32[]{:S(2)}, u32[]{:S(2)}) collective-permute-start(bf16[1536,256]{1,0:T(8,128)(2,1)S(1)} %slice.111), channel_id=1, source_target_pairs={{0,4},{1,13},{2,6},{3,15},{4,8},{5,1},{6,10},{7,3},{8,12},{9,5},{1... | collective-permute-start | bytes 2359304 | tf_op jit(solution)/shard_map/ppermute | solution.py:26
  62.6 69.3 %copy-start.2 = (bf16[1536,1024]{1,0:T(8,128)(2,1)}, bf16[1536,1024]{1,0:T(8,128)(2,1)S(1)}, u32[]{:S(2)}) copy-start(bf16[1536,1024]{1,0:T(8,128)(2,1)S(1)} %pad_maximum_fusion.1) | copy-start | bytes 9437188
  68.0 57.1 %collective-permute-start.26 = (bf16[256,1024]{1,0:T(8,128)(2,1)S(1)}, bf16[256,1024]{1,0:T(8,128)(2,1)S(1)}, u32[]{:S(2)}, u32[]{:S(2)}) collective-permute-start(bf16[256,1024]{1,0:T(8,128)(2,1)S(1)} %convolution_convert_fusion.10), channel_id=1, source_target_pairs={{0,32},{1,97},{2,34},{3,99},{4,36},{5,101},{6,38},{7,103},{8,40},{... | collective-permute-start | bytes 1572872 | tf_op jit(solution)/shard_map/ppermute | solution.py:26
  73.0 21.4 %collective-permute-start.27 = (bf16[272,1024]{1,0:T(8,128)(2,1)S(1)}, bf16[272,1024]{1,0:T(8,128)(2,1)S(1)}, u32[]{:S(2)}, u32[]{:S(2)}) collective-permute-start(bf16[272,1024]{1,0:T(8,128)(2,1)S(1)} %pad_maximum_fusion.7), channel_id=1, source_target_pairs={{0,32},{1,97},{2,34},{3,99},{4,36},{5,101},{6,38},{7,103},{8,40},{... | collective-permute-start | bytes 1671176 | tf_op jit(solution)/shard_map/ppermute | solution.py:26
  73.1 25.2 %collective-permute-start.33 = (bf16[1536,256]{1,0:T(8,128)(2,1)S(1)}, bf16[1536,256]{1,0:T(8,128)(2,1)S(1)}, u32[]{:S(2)}, u32[]{:S(2)}) collective-permute-start(bf16[1536,256]{1,0:T(8,128)(2,1)S(1)} %collective-permute-done.17), channel_id=1, source_target_pairs={{0,1},{1,0},{2,3},{3,2},{4,5},{5,4},{6,7},{7,6},{8,9},{9,8},{10,11... | collective-permute-start | bytes 2359304 | tf_op jit(solution)/shard_map/ppermute | solution.py:26
  73.3 25.4 %collective-permute-start.32 = (bf16[1536,256]{1,0:T(8,128)(2,1)S(1)}, bf16[1536,256]{1,0:T(8,128)(2,1)S(1)}, u32[]{:S(2)}, u32[]{:S(2)}) collective-permute-start(bf16[1536,256]{1,0:T(8,128)(2,1)S(1)} %collective-permute-done.16), channel_id=1, source_target_pairs={{0,1},{1,0},{2,3},{3,2},{4,5},{5,4},{6,7},{7,6},{8,9},{9,8},{10,11... | collective-permute-start | bytes 2359304 | tf_op jit(solution)/shard_map/ppermute | solution.py:26
  75.2 15.0 %collective-permute-start.23 = (bf16[256,1024]{1,0:T(8,128)(2,1)S(1)}, bf16[256,1024]{1,0:T(8,128)(2,1)S(1)}, u32[]{:S(2)}, u32[]{:S(2)}) collective-permute-start(bf16[256,1024]{1,0:T(8,128)(2,1)S(1)} %convolution_convert_fusion.6), channel_id=1, source_target_pairs={{0,32},{1,97},{2,34},{3,99},{4,36},{5,101},{6,38},{7,103},{8,40},{... | collective-permute-start | bytes 1572872 | tf_op jit(solution)/shard_map/ppermute | solution.py:26
  90.1 25.4 %collective-permute-start.11 = (bf16[1024,512]{1,0:T(8,128)(2,1)S(1)}, bf16[1024,512]{1,0:T(8,128)(2,1)S(1)}, u32[]{:S(2)}, u32[]{:S(2)}) collective-permute-start(bf16[1024,512]{1,0:T(8,128)(2,1)S(1)} %slice.139), channel_id=1, source_target_pairs={{0,18},{1,19},{2,16},{3,17},{4,22},{5,23},{6,20},{7,21},{8,26},{9,... | collective-permute-start | bytes 3145736 | tf_op jit(solution)/shard_map/ppermute | solution.py:26
  94.5 25.8 %collective-permute-start.22 = (bf16[256,1024]{1,0:T(8,128)(2,1)S(1)}, bf16[256,1024]{1,0:T(8,128)(2,1)S(1)}, u32[]{:S(2)}, u32[]{:S(2)}) collective-permute-start(bf16[256,1024]{1,0:T(8,128)(2,1)S(1)} %convolution_convert_fusion.8), channel_id=1, source_target_pairs={{0,32},{1,97},{2,34},{3,99},{4,36},{5,101},{6,38},{7,103},{8,40},{... | collective-permute-start | bytes 1572872 | tf_op jit(solution)/shard_map/ppermute | solution.py:26
  98.4 21.9 %collective-permute-start.24 = (bf16[256,1024]{1,0:T(8,128)(2,1)S(1)}, bf16[256,1024]{1,0:T(8,128)(2,1)S(1)}, u32[]{:S(2)}, u32[]{:S(2)}) collective-permute-start(bf16[256,1024]{1,0:T(8,128)(2,1)S(1)} %add_convert_fusion.2), channel_id=1, source_target_pairs={{0,96},{1,33},{2,98},{3,35},{4,100},{5,37},{6,102},{7,39},{8,104},... | collective-permute-start | bytes 1572872 | tf_op jit(solution)/shard_map/ppermute | solution.py:26
  98.7 24.7 %collective-permute-start.28 = (bf16[272,1024]{1,0:T(8,128)(2,1)S(1)}, bf16[272,1024]{1,0:T(8,128)(2,1)S(1)}, u32[]{:S(2)}, u32[]{:S(2)}) collective-permute-start(bf16[272,1024]{1,0:T(8,128)(2,1)S(1)} %pad_maximum_fusion.8), channel_id=1, source_target_pairs={{0,96},{1,33},{2,98},{3,35},{4,100},{5,37},{6,102},{7,39},{8,104},... | collective-permute-start | bytes 1671176 | tf_op jit(solution)/shard_map/ppermute | solution.py:26
  100.6 31.4 %copy-start.3 = (bf16[4,1536,256]{2,1,0:T(8,128)(2,1)}, bf16[4,1536,256]{2,1,0:T(8,128)(2,1)S(1)}, u32[]{:S(2)}) copy-start(bf16[4,1536,256]{2,1,0:T(8,128)(2,1)S(1)} %pad_maximum_fusion.4) | copy-start | bytes 9437188
  115.6 22.9 %collective-permute-start.34 = (bf16[256,1024]{1,0:T(8,128)(2,1)}, bf16[256,1024]{1,0:T(8,128)(2,1)}, u32[]{:S(2)}, u32[]{:S(2)}) collective-permute-start(bf16[256,1024]{1,0:T(8,128)(2,1)} %convolution_convert_fusion.2), channel_id=1, source_target_pairs={{0,32},{1,97},{2,34},{3,99},{4,36},{5,101},{6,38},{7,103},{8,40},{... | collective-permute-start | bytes 1572872 | tf_op jit(solution)/shard_map/ppermute | solution.py:26
  120.3 11.6 %collective-permute-start.35 = (bf16[256,1024]{1,0:T(8,128)(2,1)S(1)}, bf16[256,1024]{1,0:T(8,128)(2,1)S(1)}, u32[]{:S(2)}, u32[]{:S(2)}) collective-permute-start(bf16[256,1024]{1,0:T(8,128)(2,1)S(1)} %convolution_convert_fusion), channel_id=1, source_target_pairs={{0,32},{1,97},{2,34},{3,99},{4,36},{5,101},{6,38},{7,103},{8,40},{... | collective-permute-start | bytes 1572872 | tf_op jit(solution)/shard_map/ppermute | solution.py:26
  120.3 27.4 %collective-permute-start.12 = (bf16[1024,512]{1,0:T(8,128)(2,1)}, bf16[1024,512]{1,0:T(8,128)(2,1)}, u32[]{:S(2)}, u32[]{:S(2)}) collective-permute-start(bf16[1024,512]{1,0:T(8,128)(2,1)} %broadcast_select_fusion), channel_id=1, source_target_pairs={{0,16},{1,17},{2,18},{3,19},{4,20},{5,21},{6,22},{7,23},{8,24},{9,... | collective-permute-start | bytes 3145736 | tf_op jit(solution)/shard_map/ppermute | solution.py:26
  123.4 10.4 %collective-permute-start.25 = (bf16[256,512]{1,0:T(8,128)(2,1)}, bf16[256,512]{1,0:T(8,128)(2,1)S(1)}, u32[]{:S(2)}, u32[]{:S(2)}) collective-permute-start(bf16[256,512]{1,0:T(8,128)(2,1)} %slice.199), channel_id=1, source_target_pairs={{0,18},{1,19},{2,16},{3,17},{4,22},{5,23},{6,20},{7,21},{8,26},{9,... | collective-permute-start | bytes 786440 | tf_op jit(solution)/shard_map/ppermute | solution.py:26
  126.2 7.6 %copy-start.4 = (f32[256,1024]{1,0:T(8,128)}, f32[256,1024]{1,0:T(8,128)S(1)}, u32[]{:S(2)}) copy-start(f32[256,1024]{1,0:T(8,128)S(1)} %convert_add_fusion.2) | copy-start | bytes 3145732
  127.0 10.2 %collective-permute-start.29 = (bf16[256,512]{1,0:T(8,128)(2,1)}, bf16[256,512]{1,0:T(8,128)(2,1)}, u32[]{:S(2)}, u32[]{:S(2)}) collective-permute-start(bf16[256,512]{1,0:T(8,128)(2,1)} %slice.198), channel_id=1, source_target_pairs={{0,18},{1,19},{2,16},{3,17},{4,22},{5,23},{6,20},{7,21},{8,26},{9,... | collective-permute-start | bytes 786440 | tf_op jit(solution)/shard_map/ppermute | solution.py:26
  133.7 8.6 %collective-permute-start.36 = (bf16[256,1024]{1,0:T(8,128)(2,1)}, bf16[256,1024]{1,0:T(8,128)(2,1)}, u32[]{:S(2)}, u32[]{:S(2)}) collective-permute-start(bf16[256,1024]{1,0:T(8,128)(2,1)} %add_convert_fusion), channel_id=1, source_target_pairs={{0,96},{1,33},{2,98},{3,35},{4,100},{5,37},{6,102},{7,39},{8,104},... | collective-permute-start | bytes 1572872 | tf_op jit(solution)/shard_map/ppermute | solution.py:26
  134.9 22.0 %collective-permute-start.31 = (bf16[256,512]{1,0:T(8,128)(2,1)S(1)}, bf16[256,512]{1,0:T(8,128)(2,1)S(1)}, u32[]{:S(2)}, u32[]{:S(2)}) collective-permute-start(bf16[256,512]{1,0:T(8,128)(2,1)S(1)} %fusion.50), channel_id=1, source_target_pairs={{0,16},{1,17},{2,18},{3,19},{4,20},{5,21},{6,22},{7,23},{8,24},{9,... | collective-permute-start | bytes 786440 | tf_op jit(solution)/shard_map/ppermute | solution.py:26
  145.8 7.5 %collective-permute-start.37 = (bf16[256,512]{1,0:T(8,128)(2,1)S(1)}, bf16[256,512]{1,0:T(8,128)(2,1)S(1)}, u32[]{:S(2)}, u32[]{:S(2)}) collective-permute-start(bf16[256,512]{1,0:T(8,128)(2,1)S(1)} %slice.197), channel_id=1, source_target_pairs={{0,18},{1,19},{2,16},{3,17},{4,22},{5,23},{6,20},{7,21},{8,26},{9,... | collective-permute-start | bytes 786440 | tf_op jit(solution)/shard_map/ppermute | solution.py:26
  149.5 16.8 %copy-start.7 = (f32[512]{0:T(512)S(1)}, f32[512]{0:T(512)}, u32[]{:S(2)}) copy-start(f32[512]{0:T(512)} %param.9) | copy-start | bytes 6148
  149.5 17.5 %copy-start.5 = (f32[256,1024]{1,0:T(8,128)S(1)}, f32[256,1024]{1,0:T(8,128)}, u32[]{:S(2)}) copy-start(f32[256,1024]{1,0:T(8,128)} %copy-done.4) | copy-start | bytes 3145732
  149.5 6.5 %collective-permute-start.14 = (bf16[256,512]{1,0:T(8,128)(2,1)S(1)}, bf16[256,512]{1,0:T(8,128)(2,1)S(1)}, u32[]{:S(2)}, u32[]{:S(2)}) collective-permute-start(bf16[256,512]{1,0:T(8,128)(2,1)S(1)} %get-tuple-element.40), channel_id=1, source_target_pairs={{0,32},{1,97},{2,34},{3,99},{4,36},{5,101},{6,38},{7,103},{8,40},{... | collective-permute-start | bytes 786440 | tf_op jit(solution)/shard_map/ppermute | solution.py:26
  152.2 8.8 %collective-permute-start.30 = (bf16[272,512]{1,0:T(8,128)(2,1)S(1)}, bf16[272,512]{1,0:T(8,128)(2,1)S(1)}, u32[]{:S(2)}, u32[]{:S(2)}) collective-permute-start(bf16[272,512]{1,0:T(8,128)(2,1)S(1)} %fusion.49), channel_id=1, source_target_pairs={{0,16},{1,17},{2,18},{3,19},{4,20},{5,21},{6,22},{7,23},{8,24},{9,... | collective-permute-start | bytes 835592 | tf_op jit(solution)/shard_map/ppermute | solution.py:26
  153.4 12.9 %collective-permute-start.38 = (bf16[256,512]{1,0:T(8,128)(2,1)S(1)}, bf16[256,512]{1,0:T(8,128)(2,1)S(1)}, u32[]{:S(2)}, u32[]{:S(2)}) collective-permute-start(bf16[256,512]{1,0:T(8,128)(2,1)S(1)} %fusion.52), channel_id=1, source_target_pairs={{0,16},{1,17},{2,18},{3,19},{4,20},{5,21},{6,22},{7,23},{8,24},{9,... | collective-permute-start | bytes 786440 | tf_op jit(solution)/shard_map/ppermute | solution.py:26
  153.9 15.3 %collective-permute-start.13 = (bf16[256,512]{1,0:T(8,128)(2,1)S(1)}, bf16[256,512]{1,0:T(8,128)(2,1)S(1)}, u32[]{:S(2)}, u32[]{:S(2)}) collective-permute-start(bf16[256,512]{1,0:T(8,128)(2,1)S(1)} %get-tuple-element.39), channel_id=1, source_target_pairs={{0,32},{1,97},{2,34},{3,99},{4,36},{5,101},{6,38},{7,103},{8,40},{... | collective-permute-start | bytes 786440 | tf_op jit(solution)/shard_map/ppermute | solution.py:26
  156.1 13.1 %collective-permute-start.15 = (bf16[256,512]{1,0:T(8,128)(2,1)S(1)}, bf16[256,512]{1,0:T(8,128)(2,1)S(1)}, u32[]{:S(2)}, u32[]{:S(2)}) collective-permute-start(bf16[256,512]{1,0:T(8,128)(2,1)S(1)} %fusion.47), channel_id=1, source_target_pairs={{0,96},{1,33},{2,98},{3,35},{4,100},{5,37},{6,102},{7,39},{8,104},... | collective-permute-start | bytes 786440 | tf_op jit(solution)/shard_map/ppermute | solution.py:26
